TPU v7x, 32 devices: a whole 2x2x4 slice. The times are simulated.
32 devices in a mesh: dp: 8 (over z, y), tensor: 4 (over x, core).
Axes of the slice: x: 2, y: 2, z: 4, core: 2. Of those that a mesh axis runs over, the one named last changes fastest.
Arguments:
- tokens: bfloat16 [16384, 1024], P(('dp', 'tensor')), may hold values from -6 to 6
- output_cotangent: bfloat16 [16384, 1024], P(('dp', 'tensor')), may hold values from -6 to 6
- lengths: int32 [8], P('dp'), may hold values from 1024 to 2048, as said below
- block_place: int32 [8, 32], P('dp'), may hold values from 0 to 31, each once within a row
- random_blocks: int32 [8, 16, 32, 3], P('dp', 'tensor'), may hold values from 0 to 31
- qkv_weight: bfloat16 [1024, 3, 1024], P('dp', None, 'tensor'), may hold values from -0.1875 to 0.1875
- out_weight: bfloat16 [1024, 1024], P('dp', 'tensor'), may hold values from -0.75 to 0.75
- up_weight: bfloat16 [1024, 4096], P('dp', 'tensor'), may hold values from -0.1875 to 0.1875
- down_weight: bfloat16 [1024, 4096], P('dp', 'tensor'), may hold values from -0.09375 to 0.09375
- vectors: float32 [8, 1024], P(None, ('dp', 'tensor')), may hold values from -2 to 2
- hidden_bias: float32 [1, 4096], P(None, ('dp', 'tensor')), may hold values from -3 to 3
Outputs:
- output: bfloat16 [16384, 1024], P(('dp', 'tensor'))
- input_grad: bfloat16 [16384, 1024], P(('dp', 'tensor'))
- qkv_weight_grad: float32 [1024, 3, 1024], P('dp', None, 'tensor')
- out_weight_grad: float32 [1024, 1024], P('dp', 'tensor')
- up_weight_grad: float32 [1024, 4096], P('dp', 'tensor')
- down_weight_grad: float32 [1024, 4096], P('dp', 'tensor')
- vectors_grad: float32 [8, 1024], P(None, ('dp', 'tensor'))
- hidden_bias_grad: float32 [1, 4096], P(None, ('dp', 'tensor'))
Inputs may be any that keep to these rules, and one draw needn't show every extreme that they name: `lengths`: one sequence has exactly 2048 tokens. `block_place`: each row is a permutation.
All inputs are finite; a program needn't handle non-finite values.
Results may differ from a plain program's by a relative error of at most 0.015.
Values may be sent and summed in bfloat16 or wider, within the bound.
No kernel may reach another device: no remote copies, remote signals or barrier semaphores. Data moves between devices by JAX's collectives and lax.ppermute only.
A program may use at most 192 MiB of HBM per device.

v0:
```python
import math

import jax
import jax.numpy as jnp
from jax import lax
from jax.sharding import PartitionSpec as P

HEAD_DIM = 64
BLOCK = 64


EPS = 1e-05
NEGATIVE = -1e30


def in_blocks(value, dim, count):
    before, after = (value.shape[:dim], value.shape[dim + 1 :])
    return jnp.moveaxis(value.reshape(*before, count, -1, *after), dim, 0)


def sent_and_summed(value, axis, dim):
    count = lax.axis_size(axis)
    blocks = lax.all_to_all(in_blocks(value, dim, count), axis, 0, 0, tiled=True)
    return jnp.sum(blocks.astype(jnp.float32), axis=0)


def in_one_piece(arrays, axis, dim, along):
    widths = [math.prod(a.shape[along:]) for a in arrays]
    both = jnp.concatenate(
        [a.reshape(*a.shape[:along], w) for a, w in zip(arrays, widths)], axis=along
    )
    result = sent_and_summed(both, axis, dim)
    blocks = jnp.split(result, [sum(widths[:k]) for k in range(1, len(widths))], axis=along)
    return tuple(
        (b.reshape(*result.shape[:along], *a.shape[along:]) for a, b in zip(arrays, blocks))
    )


def layer_norm_parts(input_rows, gain_row, shift_row):
    centred = input_rows - jnp.mean(input_rows, axis=-1, keepdims=True)
    inverse = lax.rsqrt(jnp.mean(centred * centred, axis=-1, keepdims=True) + EPS)
    unit_rows = centred * inverse
    return (unit_rows * gain_row + shift_row, unit_rows, inverse)


def layer_norm_back(grad_normed, unit_rows, inverse, gain_row):
    grad_unit = grad_normed * gain_row
    grad_rows = inverse * (
        grad_unit
        - jnp.mean(grad_unit, axis=-1, keepdims=True)
        - unit_rows * jnp.mean(grad_unit * unit_rows, axis=-1, keepdims=True)
    )
    return (grad_rows, jnp.sum(grad_normed * unit_rows, axis=0), jnp.sum(grad_normed, axis=0))


def gelu_tanh(pre_active):
    return jax.nn.gelu(pre_active, approximate=True)


def gather_rows(local_rows):
    return lax.all_gather(local_rows, "tensor", axis=0, tiled=True)


def sum_rows(partial_rows):
    return lax.psum_scatter(
        partial_rows.astype(jnp.bfloat16), "tensor", scatter_dimension=0, tiled=True
    ).astype(jnp.float32)


def attention_weights(qkv_weight, out_weight):
    return (
        lax.all_gather(qkv_weight, "dp", axis=0, tiled=True),
        lax.all_gather(out_weight, "dp", axis=0, tiled=True),
    )


def feed_weights(up_weight, down_weight):
    return (
        lax.all_gather(up_weight, "dp", axis=0, tiled=True),
        lax.all_gather(down_weight, "dp", axis=0, tiled=True),
    )


def block_masks(length, placing, chosen):
    nblocks = (length + BLOCK - 1) // BLOCK
    query_seq = placing[:, None]
    key_seq = placing[None, :]
    common = (
        (query_seq == 0)
        | (query_seq == nblocks - 1)
        | (key_seq == 0)
        | (key_seq == nblocks - 1)
        | (jnp.abs(query_seq - key_seq) <= 1)
    )
    by_query = jnp.take(chosen, placing, axis=1)
    random_hit = jnp.any(by_query[:, :, None, :] == key_seq[None, :, :, None], axis=-1)
    allowed = common[None] | random_hit
    positions = placing[:, None] * BLOCK + jnp.arange(BLOCK, dtype=jnp.int32)[None, :]
    return (allowed, positions < length)


def tile_scores(query_tile, key_rows, allowed_tile, key_valid, score_scale):
    scores = (
        jnp.einsum("qhd,khd->hqk", query_tile, key_rows, preferred_element_type=jnp.float32)
        * score_scale
    )
    heads_here = allowed_tile.shape[0]
    blocks_here = allowed_tile.shape[1]
    block_size = key_valid.shape[1]
    scores = scores.reshape(heads_here, blocks_here, block_size, key_valid.shape[0], block_size)
    keep_mask = allowed_tile[:, :, None, :, None] & key_valid[None, None, None, :, :]
    scores = jnp.where(keep_mask, scores, NEGATIVE)
    return scores.reshape(heads_here, blocks_here * block_size, -1)


def project_heads(normed_all, qkv_full, bias_query, bias_value):
    projected = jnp.einsum("td,dcf->ctf", normed_all, qkv_full, preferred_element_type=jnp.float32)
    head_shape = (normed_all.shape[0], -1, HEAD_DIM)
    queries = (projected[0] + bias_query).astype(jnp.bfloat16).reshape(head_shape)
    key_rows = projected[1].astype(jnp.bfloat16).reshape(head_shape)
    value_rows = (projected[2] + bias_value).astype(jnp.bfloat16).reshape(head_shape)
    return (queries, key_rows, value_rows)


def attend(queries, key_rows, value_rows, allowed, key_valid, tile_rows, score_scale):
    per_tile = tile_rows // BLOCK

    def one_tile(number):
        query_tile = lax.dynamic_slice_in_dim(queries, number * tile_rows, tile_rows, 0)
        allowed_tile = lax.dynamic_slice_in_dim(allowed, number * per_tile, per_tile, 1)
        scores = tile_scores(query_tile, key_rows, allowed_tile, key_valid, score_scale)
        row_top = jnp.max(scores, axis=-1, keepdims=True)
        weights = jnp.exp(scores - row_top)
        row_total = jnp.sum(weights, axis=-1, keepdims=True)
        probabilities = (weights / row_total).astype(jnp.bfloat16)
        context_tile = jnp.einsum(
            "hqk,khd->qhd", probabilities, value_rows, preferred_element_type=jnp.float32
        )
        return (
            context_tile.reshape(tile_rows, -1).astype(jnp.bfloat16),
            (row_top + jnp.log(row_total))[..., 0],
        )

    context_tiles, log_totals = lax.map(
        one_tile, jnp.arange(queries.shape[0] // tile_rows, dtype=jnp.int32)
    )
    return (context_tiles.reshape(queries.shape[0], -1), log_totals)


def attend_back(
    queries,
    key_rows,
    value_rows,
    grad_context,
    log_totals,
    allowed,
    key_valid,
    tile_rows,
    score_scale,
):
    per_tile = tile_rows // BLOCK

    def one_tile(state_pair, number):
        grad_keys, grad_values = state_pair
        query_tile = lax.dynamic_slice_in_dim(queries, number * tile_rows, tile_rows, 0)
        grad_tile = lax.dynamic_slice_in_dim(grad_context, number * tile_rows, tile_rows, 0)
        allowed_tile = lax.dynamic_slice_in_dim(allowed, number * per_tile, per_tile, 1)
        scores = tile_scores(query_tile, key_rows, allowed_tile, key_valid, score_scale)
        probabilities = jnp.exp(scores - log_totals[number][:, :, None])
        probs_low = probabilities.astype(jnp.bfloat16)
        grad_probs = jnp.einsum(
            "qhd,khd->hqk", grad_tile, value_rows, preferred_element_type=jnp.float32
        )
        row_inner = jnp.sum(probabilities * grad_probs, axis=-1, keepdims=True)
        grad_scores = (probabilities * (grad_probs - row_inner)).astype(jnp.bfloat16)
        grad_query = (
            jnp.einsum("hqk,khd->qhd", grad_scores, key_rows, preferred_element_type=jnp.float32)
            * score_scale
        )
        grad_keys = (
            grad_keys
            + jnp.einsum(
                "hqk,qhd->khd", grad_scores, query_tile, preferred_element_type=jnp.float32
            )
            * score_scale
        )
        grad_values = grad_values + jnp.einsum(
            "hqk,qhd->khd", probs_low, grad_tile, preferred_element_type=jnp.float32
        )
        return ((grad_keys, grad_values), grad_query.astype(jnp.bfloat16))

    zero_state = jnp.zeros(key_rows.shape, jnp.float32)
    final_state, grad_queries = lax.scan(
        one_tile,
        (zero_state, zero_state),
        jnp.arange(queries.shape[0] // tile_rows, dtype=jnp.int32),
    )
    flat_queries = grad_queries.reshape(queries.shape[0], -1)
    flat_keys = final_state[0].reshape(flat_queries.shape).astype(jnp.bfloat16)
    flat_values = final_state[1].reshape(flat_queries.shape).astype(jnp.bfloat16)
    return (flat_queries, flat_keys, flat_values)


def per_device(
    tokens,
    output_cotangent,
    lengths,
    block_place,
    random_blocks,
    qkv_weight,
    out_weight,
    up_weight,
    down_weight,
    vectors,
    hidden_bias,
):
    vectors_full, hidden_full = (
        lax.all_gather(vectors, ("dp", "tensor"), axis=1, tiled=True),
        lax.all_gather(hidden_bias, ("dp", "tensor"), axis=1, tiled=True),
    )
    width_local = qkv_weight.shape[2]
    units_local = up_weight.shape[1]
    position = lax.axis_index("tensor")
    head_start = position * width_local
    unit_start = position * units_local
    bias_query = lax.dynamic_slice_in_dim(vectors_full[6], head_start, width_local)
    bias_value = lax.dynamic_slice_in_dim(vectors_full[7], head_start, width_local)
    bias_hidden = lax.dynamic_slice_in_dim(hidden_full[0], unit_start, units_local)
    allowed, key_valid = block_masks(lengths[0], block_place[0], random_blocks[0])
    slot_rows = tokens.shape[0] * lax.axis_size("tensor")
    tile_rows = min(512, slot_rows)
    score_scale = HEAD_DIM ** (-0.5)
    residual_in = tokens.astype(jnp.float32)
    qkv_full, out_full = attention_weights(qkv_weight, out_weight)
    normed_one, unit_one, inverse_one = layer_norm_parts(
        residual_in, vectors_full[0], vectors_full[1]
    )
    normed_one_all = gather_rows(normed_one.astype(jnp.bfloat16))
    queries, key_rows, value_rows = project_heads(normed_one_all, qkv_full, bias_query, bias_value)
    context, log_totals = attend(
        queries, key_rows, value_rows, allowed, key_valid, tile_rows, score_scale
    )
    attended = sum_rows(
        jnp.einsum("tf,df->td", context, out_full, preferred_element_type=jnp.float32)
    )
    middle = residual_in + attended + vectors_full[4]
    normed_two, unit_two, inverse_two = layer_norm_parts(middle, vectors_full[2], vectors_full[3])
    up_full, down_full = feed_weights(up_weight, down_weight)
    normed_two_all = gather_rows(normed_two.astype(jnp.bfloat16))
    hidden = jnp.dot(normed_two_all, up_full, preferred_element_type=jnp.float32) + bias_hidden
    active = gelu_tanh(hidden).astype(jnp.bfloat16)
    feed_out = sum_rows(
        jnp.einsum("tf,df->td", active, down_full, preferred_element_type=jnp.float32)
    )
    output = (middle + feed_out + vectors_full[5]).astype(jnp.bfloat16)
    grad_all = gather_rows(output_cotangent)
    up_back, down_back = feed_weights(up_weight, down_weight)
    normed_two_back = gather_rows(normed_two.astype(jnp.bfloat16))
    hidden_back = (
        jnp.dot(normed_two_back, up_back, preferred_element_type=jnp.float32) + bias_hidden
    )
    active_back = gelu_tanh(hidden_back).astype(jnp.bfloat16)
    grad_active = jnp.dot(grad_all, down_back, preferred_element_type=jnp.float32)
    gelu_pullback = jax.vjp(gelu_tanh, hidden_back)[1]
    grad_hidden = gelu_pullback(grad_active)[0].astype(jnp.bfloat16)
    grad_up = jnp.einsum(
        "td,tf->df", normed_two_back, grad_hidden, preferred_element_type=jnp.float32
    )
    grad_down = jnp.einsum("td,tf->df", grad_all, active_back, preferred_element_type=jnp.float32)
    grad_bias_hidden = jnp.sum(grad_hidden, axis=0, dtype=jnp.float32)
    grad_normed_two = sum_rows(
        jnp.einsum("tf,df->td", grad_hidden, up_back, preferred_element_type=jnp.float32)
    )
    up_weight_grad, down_weight_grad = (
        lax.psum_scatter(grad_up, "dp", scatter_dimension=0, tiled=True),
        lax.psum_scatter(grad_down, "dp", scatter_dimension=0, tiled=True),
    )
    cotangent_rows = output_cotangent.astype(jnp.float32)
    grad_middle_part, grad_gain_two, grad_shift_two = layer_norm_back(
        grad_normed_two, unit_two, inverse_two, vectors_full[2]
    )
    grad_middle = cotangent_rows + grad_middle_part
    grad_attended_all = gather_rows(grad_middle.astype(jnp.bfloat16))
    qkv_back, out_back = attention_weights(qkv_weight, out_weight)
    normed_one_back = gather_rows(normed_one.astype(jnp.bfloat16))
    queries_back, keys_back, values_back = project_heads(
        normed_one_back, qkv_back, bias_query, bias_value
    )
    grad_context = jnp.dot(grad_attended_all, out_back, preferred_element_type=jnp.float32).astype(
        jnp.bfloat16
    )
    grad_out_weight = jnp.einsum(
        "td,tf->df", grad_attended_all, context, preferred_element_type=jnp.float32
    )
    grad_context_heads = grad_context.reshape(slot_rows, -1, HEAD_DIM)
    grad_queries, grad_keys, grad_values = attend_back(
        queries_back,
        keys_back,
        values_back,
        grad_context_heads,
        log_totals,
        allowed,
        key_valid,
        tile_rows,
        score_scale,
    )
    grad_projected = jnp.stack([grad_queries, grad_keys, grad_values])
    grad_qkv = jnp.einsum(
        "td,ctf->dcf", normed_one_back, grad_projected, preferred_element_type=jnp.float32
    )
    grad_normed_one = sum_rows(
        jnp.einsum("ctf,dcf->td", grad_projected, qkv_back, preferred_element_type=jnp.float32)
    )
    qkv_weight_grad, out_weight_grad = in_one_piece(
        (grad_qkv.astype(jnp.bfloat16), grad_out_weight.astype(jnp.bfloat16)), "dp", 0, 1
    )
    grad_input_part, grad_gain_one, grad_shift_one = layer_norm_back(
        grad_normed_one, unit_one, inverse_one, vectors_full[0]
    )
    input_grad = (grad_middle + grad_input_part).astype(jnp.bfloat16)
    local_grads = jnp.stack(
        [
            grad_gain_one,
            grad_shift_one,
            grad_gain_two,
            grad_shift_two,
            jnp.sum(grad_middle, axis=0),
            jnp.sum(cotangent_rows, axis=0),
        ]
    )
    head_bias_grads = jnp.stack(
        [
            jnp.sum(grad_queries, axis=0, dtype=jnp.float32),
            jnp.sum(grad_values, axis=0, dtype=jnp.float32),
        ]
    )
    head_grads = lax.dynamic_update_slice(
        jnp.zeros((2, vectors_full.shape[1]), jnp.float32), head_bias_grads, (0, head_start)
    )
    hidden_grads = lax.dynamic_update_slice(
        jnp.zeros(hidden_full.shape, jnp.float32), grad_bias_hidden[None, :], (0, unit_start)
    )
    vectors_grad, hidden_bias_grad = (
        lax.psum_scatter(
            jnp.concatenate([local_grads, head_grads], axis=0),
            ("dp", "tensor"),
            scatter_dimension=1,
            tiled=True,
        ),
        lax.psum_scatter(hidden_grads, ("dp", "tensor"), scatter_dimension=1, tiled=True),
    )
    return (
        output,
        input_grad,
        qkv_weight_grad,
        out_weight_grad,
        up_weight_grad,
        down_weight_grad,
        vectors_grad,
        hidden_bias_grad,
    )


def solution(mesh):
    placed = (
        P(("dp", "tensor"), None),
        P(("dp", "tensor"), None),
        P("dp"),
        P("dp", None),
        P("dp", "tensor", None, None),
        P("dp", None, "tensor"),
        P("dp", "tensor"),
        P("dp", "tensor"),
        P("dp", "tensor"),
        P(None, ("dp", "tensor")),
        P(None, ("dp", "tensor")),
    )
    return jax.shard_map(
        per_device,
        mesh=mesh,
        in_specs=placed,
        out_specs=(
            P(("dp", "tensor"), None),
            P(("dp", "tensor"), None),
            P("dp", None, "tensor"),
            P("dp", "tensor"),
            P("dp", "tensor"),
            P("dp", "tensor"),
            P(None, ("dp", "tensor")),
            P(None, ("dp", "tensor")),
        ),
        check_vma=False,
    )
```

profile of v0, /device:TPU:0, one launch (start us, length us, event | category | flops | bytes accessed | tf_op | source)
XLA Modules:
  0.0 1533.9 jit_solution(7175553528561986382)
XLA Ops:
  9.1 44.2 %all-gather = f32[32,32,8]{1,2,0:T(8,128)S(1)} all-gather(f32[1,32,8]{1,2,0:T(8,128)} %bitcast.196), channel_id=1, replica_groups=mesh['dp'=8,'tensor'=4] {'dp','tensor'}, dimensions={0}, use_global_device_ids=true | all-gather | bytes 33792 | tf_op jit(solution)/shard_map/all_gather | solution.py:218
  62.7 33.6 %all_gather.39 = bf16[1024,256]{1,0:T(8,128)(2,1)} all-gather(bf16[128,256]{1,0:T(8,128)(2,1)S(1)} %copy-done.18), channel_id=1, replica_groups=mesh['dp'=8,'tensor'=4] {'dp'}, dimensions={0}, use_global_device_ids=true | all-gather | bytes 589824 | tf_op jit(solution)/shard_map/all_gather | solution.py:73
  96.2 5.7 fusion.46
  104.0 192.3 %while.28 = (s32[]{:T(128)}, bf16[4,512,256]{2,1,0:T(8,128)(2,1)}, f32[4,4,512]{2,1,0:T(4,128)S(1)}, s32[4]{0:T(128)S(1)}, pred[4,32,32]{2,1,0:T(8,128)(4,1)S(1)...) while((s32[]{:T(128)}, bf16[4,512,256]{2,1,0:T(8,128)(2,1)}, ...), condition=%wide.region_6.7_spmd.clone, body=%wide.region_3.6_spmd.clone.sunk | while | flops 1124272128 | bytes 96148904 | solution.py:144
  106.8 5.4 broadcast_in_dim.120
  112.2 22.8 %broadcast_in_dim.121 = pred[4,512,2048]{2,1,0:T(32,128)(4,1)} reshape(pred[4,8,64,32,64]{4,3,2,1,0:T(32,128)(4,1)} %broadcast_in_dim.120) | data formatting | bytes 8388608 | tf_op jit(solution)/shard_map/while/body/eval_jaxpr/jit(_where)/broadcast_in_dim | solution.py:112
  135.0 5.6 fusion.134
  140.6 4.7 fusion.135
  145.4 5.8 fusion.136
  154.9 5.4 broadcast_in_dim.120
  160.2 22.8 %broadcast_in_dim.121 = pred[4,512,2048]{2,1,0:T(32,128)(4,1)} reshape(pred[4,8,64,32,64]{4,3,2,1,0:T(32,128)(4,1)} %broadcast_in_dim.120) | data formatting | bytes 8388608 | tf_op jit(solution)/shard_map/while/body/eval_jaxpr/jit(_where)/broadcast_in_dim | solution.py:112
  183.1 5.6 fusion.134
  193.4 5.8 fusion.136
  203.0 5.4 broadcast_in_dim.120
  208.3 22.8 %broadcast_in_dim.121 = pred[4,512,2048]{2,1,0:T(32,128)(4,1)} reshape(pred[4,8,64,32,64]{4,3,2,1,0:T(32,128)(4,1)} %broadcast_in_dim.120) | data formatting | bytes 8388608 | tf_op jit(solution)/shard_map/while/body/eval_jaxpr/jit(_where)/broadcast_in_dim | solution.py:112
  231.2 5.6 fusion.134
  241.5 5.8 fusion.136
  251.0 5.4 broadcast_in_dim.120
  256.4 22.8 %broadcast_in_dim.121 = pred[4,512,2048]{2,1,0:T(32,128)(4,1)} reshape(pred[4,8,64,32,64]{4,3,2,1,0:T(32,128)(4,1)} %broadcast_in_dim.120) | data formatting | bytes 8388608 | tf_op jit(solution)/shard_map/while/body/eval_jaxpr/jit(_where)/broadcast_in_dim | solution.py:112
  279.2 5.6 fusion.134
  289.6 5.8 fusion.136
  301.6 41.8 %reduce-scatter.13.cloned.1.call-done = bf16[512,1024]{1,0:T(8,128)(2,1)} async-done(((bf16[2048,1024]{1,0:T(8,128)(2,1)}), bf16[512,1024]{1,0:T(8,128)(2,1)}) %reduce-scatter.13.cloned.1.call-update) | async-done | bytes 1048592 | tf_op jit(solution)/shard_map/reduce_scatter | solution.py:65
  349.9 40.5 %all_gather.42 = f32[1,4096]{1,0:T(1,128)S(1)} all-gather(f32[1,128]{1,0:T(1,128)S(1)} %copy-done.36), channel_id=1, replica_groups=mesh['dp'=8,'tensor'=4] {'dp','tensor'}, dimensions={1}, use_global_device_ids=true | all-gather | bytes 16896 | tf_op jit(solution)/shard_map/all_gather | solution.py:219
  394.9 35.1 %all-gather.13.cloned.1.call-done = bf16[2048,1024]{1,0:T(8,128)(2,1)} async-done(((bf16[512,1024]{1,0:T(8,128)(2,1)}), bf16[2048,1024]{1,0:T(8,128)(2,1)}) %all-gather.13.cloned.1.call-update) | async-done | bytes 4194320 | tf_op jit(solution)/shard_map/all_gather | solution.py:61
  430.0 10.6 fusion.87
  440.6 40.9 %all-gather.17.cloned.1.call-done = bf16[1024,1024]{1,0:T(8,128)(2,1)} async-done(((bf16[128,1024]{1,0:T(8,128)(2,1)}), bf16[1024,1024]{1,0:T(8,128)(2,1)}) %all-gather.17.cloned.1.call-update) | async-done | bytes 2097168 | tf_op jit(solution)/shard_map/all_gather | solution.py:80
  481.5 34.6 %all-gather.19.cloned.1.call-done = bf16[2048,1024]{1,0:T(8,128)(2,1)} async-done(((bf16[512,1024]{1,0:T(8,128)(2,1)}), bf16[2048,1024]{1,0:T(8,128)(2,1)}) %all-gather.19.cloned.1.call-update) | async-done | bytes 4194320 | tf_op jit(solution)/shard_map/all_gather | solution.py:61
  516.1 14.3 convert_reduce_fusion
  532.5 6.4 convolution_convert_fusion.1
  539.3 11.7 convolution_convert_fusion.2
  551.1 32.4 %reduce-scatter.17.cloned.1.call-done = bf16[512,1024]{1,0:T(8,128)(2,1)} async-done(((bf16[2048,1024]{1,0:T(8,128)(2,1)}), bf16[512,1024]{1,0:T(8,128)(2,1)}) %reduce-scatter.17.cloned.1.call-update) | async-done | bytes 1048592 | tf_op jit(solution)/shard_map/reduce_scatter | solution.py:65
  586.8 43.7 %reduce-scatter.15.cloned.1.call-done = bf16[512,1024]{1,0:T(8,128)(2,1)} async-done(((bf16[2048,1024]{1,0:T(8,128)(2,1)}), bf16[512,1024]{1,0:T(8,128)(2,1)}) %reduce-scatter.15.cloned.1.call-update) | async-done | bytes 1048592 | tf_op jit(solution)/shard_map/reduce_scatter | solution.py:65
  637.7 34.6 %all-gather.21.cloned.1.call-done = bf16[2048,1024]{1,0:T(8,128)(2,1)} async-done(((bf16[512,1024]{1,0:T(8,128)(2,1)}), bf16[2048,1024]{1,0:T(8,128)(2,1)}) %all-gather.21.cloned.1.call-update) | async-done | bytes 4194320 | tf_op jit(solution)/shard_map/all_gather | solution.py:61
  676.7 328.6 %while.29 = (s32[]{:T(128)}, f32[2048,4,64]{0,2,1:T(8,128)}, f32[2048,4,64]{0,2,1:T(8,128)}, bf16[4,512,4,64]{1,3,2,0:T(8,128)(2,1)}, s32[4]{0:T(128)S(1)}, /*in...) while((s32[]{:T(128)}, f32[2048,4,64]{0,2,1:T(8,128)}, ...), condition=%wide.region_16.17_spmd.clone, body=%wide.region_14.16_spmd.clone.sunk | while | flops 2725054464 | bytes 256294480 | solution.py:193
  681.5 5.4 broadcast_in_dim.122
  686.9 22.8 %broadcast_in_dim.123 = pred[4,512,2048]{2,1,0:T(32,128)(4,1)} reshape(pred[4,8,64,32,64]{4,3,2,1,0:T(32,128)(4,1)} %broadcast_in_dim.122) | data formatting | bytes 8388608 | tf_op jit(solution)/shard_map/while/body/eval_jaxpr/jit(_where)/broadcast_in_dim | solution.py:112
  709.7 9.2 fusion.146
  718.9 12.7 multiply_reduce_fusion.3
  731.6 11.5 multiply_convert_fusion.5
  763.0 5.4 broadcast_in_dim.122
  768.3 22.8 %broadcast_in_dim.123 = pred[4,512,2048]{2,1,0:T(32,128)(4,1)} reshape(pred[4,8,64,32,64]{4,3,2,1,0:T(32,128)(4,1)} %broadcast_in_dim.122) | data formatting | bytes 8388608 | tf_op jit(solution)/shard_map/while/body/eval_jaxpr/jit(_where)/broadcast_in_dim | solution.py:112
  791.2 9.2 fusion.146
  800.4 12.7 multiply_reduce_fusion.3
  813.1 11.5 multiply_convert_fusion.5
  845.2 5.4 broadcast_in_dim.122
  850.5 22.8 %broadcast_in_dim.123 = pred[4,512,2048]{2,1,0:T(32,128)(4,1)} reshape(pred[4,8,64,32,64]{4,3,2,1,0:T(32,128)(4,1)} %broadcast_in_dim.122) | data formatting | bytes 8388608 | tf_op jit(solution)/shard_map/while/body/eval_jaxpr/jit(_where)/broadcast_in_dim | solution.py:112
  873.4 9.2 fusion.146
  882.6 12.7 multiply_reduce_fusion.3
  895.3 11.5 multiply_convert_fusion.5
  927.4 5.4 broadcast_in_dim.122
  932.7 22.8 %broadcast_in_dim.123 = pred[4,512,2048]{2,1,0:T(32,128)(4,1)} reshape(pred[4,8,64,32,64]{4,3,2,1,0:T(32,128)(4,1)} %broadcast_in_dim.122) | data formatting | bytes 8388608 | tf_op jit(solution)/shard_map/while/body/eval_jaxpr/jit(_where)/broadcast_in_dim | solution.py:112
  955.6 9.2 fusion.146
  964.8 12.7 multiply_reduce_fusion.3
  977.5 11.5 multiply_convert_fusion.5
  1020.0 7.8 bitcast_convert_fusion
  1030.7 13.3 convolution_bitcast_fusion
  1044.7 27.9 %reduce-scatter.19.cloned.1.call-done = bf16[512,1024]{1,0:T(8,128)(2,1)} async-done(((bf16[2048,1024]{1,0:T(8,128)(2,1)}), bf16[512,1024]{1,0:T(8,128)(2,1)}) %reduce-scatter.19.cloned.1.call-update) | async-done | bytes 1048592 | tf_op jit(solution)/shard_map/reduce_scatter | solution.py:65
  1076.5 10.0 fusion.88
  1091.6 7.8 fusion.73
  1103.5 5.7 all-to-all-start
  1109.1 105.9 %reduce-scatter.27.cloned.1.call-done = f32[128,1]{1,0:T(8,128)} async-done(((f32[4096,1]{1,0:T(8,128)}), f32[128,1]{1,0:T(8,128)}) %reduce-scatter.27.cloned.1.call-update) | async-done | bytes 528
  1216.4 86.9 %reduce-scatter.23.cloned.1.call-done = f32[128,1024]{0,1:T(8,128)} async-done(((f32[1024,1024]{0,1:T(8,128)}), f32[128,1024]{0,1:T(8,128)}) %reduce-scatter.23.cloned.1.call-update) | async-done | bytes 524304 | tf_op jit(solution)/shard_map/reduce_scatter | solution.py:276
  1314.2 124.6 %reduce-scatter.25.cloned.1.call-done = f32[32,8]{1,0:T(8,128)} async-done(((f32[1024,8]{1,0:T(8,128)}), f32[32,8]{1,0:T(8,128)}) %reduce-scatter.25.cloned.1.call-update) | async-done | bytes 1040
  1440.2 87.0 %reduce-scatter.21.cloned.1.call-done = f32[128,1024]{1,0:T(8,128)} async-done(((f32[1024,1024]{1,0:T(8,128)}), f32[128,1024]{1,0:T(8,128)}) %reduce-scatter.21.cloned.1.call-update) | async-done | bytes 524304 | tf_op jit(solution)/shard_map/reduce_scatter | solution.py:275
  (287 shorter events, 183.6 us)
Async XLA Ops:
  7.2 54.0 %copy-start.32 = (s32[1,4,32,3]{2,1,3,0:T(4,128)S(1)}, s32[1,4,32,3]{2,1,3,0:T(4,128)}, u32[]{:S(2)}) copy-start(s32[1,4,32,3]{2,1,3,0:T(4,128)} %param.19) | copy-start | bytes 4612
  7.2 54.2 %copy-start.31 = (s32[1,32]{1,0:T(1,128)S(1)}, s32[1,32]{1,0:T(1,128)}, u32[]{:S(2)}) copy-start(s32[1,32]{1,0:T(1,128)} %param.18) | copy-start | bytes 388
  7.2 55.5 %copy-start.18 = (bf16[128,256]{1,0:T(8,128)(2,1)S(1)}, bf16[128,256]{1,0:T(8,128)(2,1)}, u32[]{:S(2)}) copy-start(bf16[128,256]{1,0:T(8,128)(2,1)} %param.21) | copy-start | bytes 196612
  7.2 89.0 %all-gather.11.cloned.1.call-start = ((), (), s32[]{:S(2)}) async-start(), calls=%async_computation.10 | async-start | bytes 1769472 | tf_op jit(solution)/shard_map/all_gather | solution.py:72
  9.0 87.2 %all-gather.9.cloned.1.call-start = ((), (), s32[]{:S(2)}) async-start(), calls=%async_computation.9 | async-start | bytes 5242880 | tf_op jit(solution)/shard_map/all_gather | solution.py:61
  54.9 2.3 copy-start.21
  60.4 282.9 %reduce-scatter.13.cloned.1.call-start = ((), (), s32[]{:S(2)}) async-start(), calls=%async_computation.11 | async-start | bytes 5242880 | tf_op jit(solution)/shard_map/reduce_scatter | solution.py:65
  104.0 192.3 %copy-start.13 = (bf16[1024,256]{1,0:T(8,128)(2,1)S(1)}, bf16[1024,256]{1,0:T(8,128)(2,1)}, u32[]{:S(2)}) copy-start(bf16[1024,256]{1,0:T(8,128)(2,1)} %all_gather.39) | copy-start | bytes 1572868
  135.0 5.6 copy-start.1
  183.1 5.6 copy-start.1
  231.2 5.6 copy-start.1
  279.2 5.6 copy-start.1
  300.7 42.6 %copy-start.3 = (bf16[512,1024]{1,0:T(8,128)(2,1)S(1)}, bf16[512,1024]{1,0:T(8,128)(2,1)}, u32[]{:S(2)}) copy-start(bf16[512,1024]{1,0:T(8,128)(2,1)} %param.15) | copy-start | bytes 3145732
  300.7 42.6 %copy-start.16 = (f32[1,1024]{1,0:T(1,128)S(1)}, f32[1,1024]{1,0:T(1,128)}, u32[]{:S(2)}) copy-start(f32[1,1024]{1,0:T(1,128)} %get-tuple-element.298) | copy-start | bytes 12292
  300.8 46.2 %copy-start.17 = (f32[1,1024]{1,0:T(1,128)S(1)}, f32[1,1024]{1,0:T(1,128)}, u32[]{:S(2)}) copy-start(f32[1,1024]{1,0:T(1,128)} %get-tuple-element.297) | copy-start | bytes 12292
  300.8 46.2 %copy-start.26 = (f32[1,1024]{1,0:T(1,128)S(1)}, f32[1,1024]{1,0:T(1,128)}, u32[]{:S(2)}) copy-start(f32[1,1024]{1,0:T(1,128)} %get-tuple-element.296) | copy-start | bytes 12292
  300.8 94.1 %all-gather.15.cloned.1.call-start = ((), (), s32[]{:S(2)}) async-start(), calls=%async_computation.13 | async-start | bytes 2359296 | tf_op jit(solution)/shard_map/all_gather | solution.py:79
  301.4 128.6 %all-gather.13.cloned.1.call-start = ((), (), s32[]{:S(2)}) async-start(), calls=%async_computation.12 | async-start | bytes 5242880 | tf_op jit(solution)/shard_map/all_gather | solution.py:61
  343.4 3.6 copy-start.8
  345.1 4.8 copy-start.36
  348.5 132.9 %all-gather.17.cloned.1.call-start = ((), (), s32[]{:S(2)}) async-start(), calls=%async_computation.14 | async-start | bytes 2359296 | tf_op jit(solution)/shard_map/all_gather | solution.py:80
  349.1 167.0 %all-gather.19.cloned.1.call-start = ((), (), s32[]{:S(2)}) async-start(), calls=%async_computation.16 | async-start | bytes 5242880 | tf_op jit(solution)/shard_map/all_gather | solution.py:61
  349.9 233.6 %reduce-scatter.17.cloned.1.call-start = ((), (), s32[]{:S(2)}) async-start(), calls=%async_computation.17 | async-start | bytes 5242880 | tf_op jit(solution)/shard_map/reduce_scatter | solution.py:65
  390.4 148.9 %copy-start.33 = (f32[1,1024]{1,0:T(1,128)}, f32[1,1024]{1,0:T(1,128)S(1)}, u32[]{:S(2)}) copy-start(f32[1,1024]{1,0:T(1,128)S(1)} %constant_dynamic-slice_fusion.2) | copy-start | bytes 12292
  516.1 16.3 %copy-start.37 = (bf16[1024,1024]{1,0:T(8,128)(2,1)S(1)}, bf16[1024,1024]{1,0:T(8,128)(2,1)}, u32[]{:S(2)}) copy-start(bf16[1024,1024]{1,0:T(8,128)(2,1)} %all-gather.15.cloned.1.call-done) | copy-start | bytes 6291460
  530.4 2.0 copy-start.38
  538.8 91.7 %reduce-scatter.15.cloned.1.call-start = ((), (), s32[]{:S(2)}) async-start(), calls=%async_computation.15 | async-start | bytes 5242880 | tf_op jit(solution)/shard_map/reduce_scatter | solution.py:65
  551.0 79.5 %copy-start.25 = (f32[1,1024]{1,0:T(1,128)S(1)}, f32[1,1024]{1,0:T(1,128)}, u32[]{:S(2)}) copy-start(f32[1,1024]{1,0:T(1,128)} %get-tuple-element.295) | copy-start | bytes 12292
  551.1 121.2 %all-gather.21.cloned.1.call-start = ((), (), s32[]{:S(2)}) async-start(), calls=%async_computation.18 | async-start | bytes 5242880 | tf_op jit(solution)/shard_map/all_gather | solution.py:61
  635.1 1.3 copy-start.9
  635.1 37.1 %copy-start.14 = (bf16[1024,256]{1,0:T(8,128)(2,1)S(1)}, bf16[1024,256]{1,0:T(8,128)(2,1)}, u32[]{:S(2)}) copy-start(bf16[1024,256]{1,0:T(8,128)(2,1)} %all_gather.39) | copy-start | bytes 1572868
  637.6 435.0 %reduce-scatter.19.cloned.1.call-start = ((), (), s32[]{:S(2)}) async-start(), calls=%async_computation.19 | async-start | bytes 5242880 | tf_op jit(solution)/shard_map/reduce_scatter | solution.py:65
  709.7 9.2 copy-start.2
  731.6 15.4 %copy-start = (f32[4,512,2048]{2,1,0:T(8,128)S(1)}, f32[4,512,2048]{2,1,0:T(8,128)}, u32[]{:S(2)}) copy-start(f32[4,512,2048]{2,1,0:T(8,128)} %get-tuple-element.455) | copy-start | bytes 50331652 | tf_op jit(solution)/shard_map/while
  750.9 3.4 copy-start.5
  757.0 1.3 copy-start.6
  791.2 9.2 copy-start.2
  813.1 15.4 %copy-start = (f32[4,512,2048]{2,1,0:T(8,128)S(1)}, f32[4,512,2048]{2,1,0:T(8,128)}, u32[]{:S(2)}) copy-start(f32[4,512,2048]{2,1,0:T(8,128)} %get-tuple-element.455) | copy-start | bytes 50331652 | tf_op jit(solution)/shard_map/while
  833.1 3.4 copy-start.5
  873.4 9.2 copy-start.2
  895.3 15.4 %copy-start = (f32[4,512,2048]{2,1,0:T(8,128)S(1)}, f32[4,512,2048]{2,1,0:T(8,128)}, u32[]{:S(2)}) copy-start(f32[4,512,2048]{2,1,0:T(8,128)} %get-tuple-element.455) | copy-start | bytes 50331652 | tf_op jit(solution)/shard_map/while
  915.3 3.4 copy-start.5
  955.6 9.2 copy-start.2
  977.5 15.4 %copy-start = (f32[4,512,2048]{2,1,0:T(8,128)S(1)}, f32[4,512,2048]{2,1,0:T(8,128)}, u32[]{:S(2)}) copy-start(f32[4,512,2048]{2,1,0:T(8,128)} %get-tuple-element.455) | copy-start | bytes 50331652 | tf_op jit(solution)/shard_map/while
  997.5 3.4 copy-start.5
  1003.6 1.3 copy-start.6
  1005.3 5.2 copy-start.11
  1008.1 9.3 copy-start.7
  1020.0 7.8 copy-start.15
  1027.9 2.8 copy-start.34
  1027.9 187.1 %reduce-scatter.27.cloned.1.call-start = ((), (), s32[]{:S(2)}) async-start(), calls=%async_computation.23 | async-start | bytes 2162688
  1030.6 272.7 %reduce-scatter.23.cloned.1.call-start = ((), (), s32[]{:S(2)}) async-start(), calls=%async_computation.21 | async-start | bytes 4718592 | tf_op jit(solution)/shard_map/reduce_scatter | solution.py:276
  1043.9 28.6 %copy-start.4 = (bf16[512,1024]{1,0:T(8,128)(2,1)S(1)}, bf16[512,1024]{1,0:T(8,128)(2,1)}, u32[]{:S(2)}) copy-start(bf16[512,1024]{1,0:T(8,128)(2,1)} %param.15) | copy-start | bytes 3145732
  1043.9 28.6 %copy-start.20 = (f32[1,1024]{1,0:T(1,128)S(1)}, f32[1,1024]{1,0:T(1,128)}, u32[]{:S(2)}) copy-start(f32[1,1024]{1,0:T(1,128)} %copy-done.19) | copy-start | bytes 12292
  1044.0 28.6 %copy-start.22 = (f32[512]{0:T(512)S(1)}, f32[512]{0:T(512)}, u32[]{:S(2)}) copy-start(f32[512]{0:T(512)} %copy-done.21) | copy-start | bytes 6148
  1044.0 28.6 %copy-start.24 = (f32[512]{0:T(512)S(1)}, f32[512]{0:T(512)}, u32[]{:S(2)}) copy-start(f32[512]{0:T(512)} %copy-done.23) | copy-start | bytes 6148
  1044.0 31.4 %copy-start.27 = (f32[1024]{0:T(1024)S(1)}, f32[1024]{0:T(1024)}, u32[]{:S(2)}) copy-start(f32[1024]{0:T(1024)} %get-tuple-element.227) | copy-start | bytes 12292
  1044.0 31.4 %copy-start.28 = (f32[1024]{0:T(1024)S(1)}, f32[1024]{0:T(1024)}, u32[]{:S(2)}) copy-start(f32[1024]{0:T(1024)} %get-tuple-element.233) | copy-start | bytes 12292
  1044.0 31.4 %copy-start.29 = (f32[1024]{0:T(1024)S(1)}, f32[1024]{0:T(1024)}, u32[]{:S(2)}) copy-start(f32[1024]{0:T(1024)} %get-tuple-element.285) | copy-start | bytes 12292
  1044.0 31.4 %copy-start.30 = (f32[1024]{0:T(1024)S(1)}, f32[1024]{0:T(1024)}, u32[]{:S(2)}) copy-start(f32[1024]{0:T(1024)} %get-tuple-element.294) | copy-start | bytes 12292
  1044.0 394.8 %reduce-scatter.25.cloned.1.call-start = ((), (), s32[]{:S(2)}) async-start(), calls=%async_computation.22 | async-start | bytes 540672
  1076.5 450.7 %reduce-scatter.21.cloned.1.call-start = ((), (), s32[]{:S(2)}) async-start(), calls=%async_computation.20 | async-start | bytes 4718592 | tf_op jit(solution)/shard_map/reduce_scatter | solution.py:275
  1103.5 207.8 %copy-start.10 = (f32[512,1024]{1,0:T(8,128)S(1)}, f32[512,1024]{1,0:T(8,128)}, u32[]{:S(2)}) copy-start(f32[512,1024]{1,0:T(8,128)} %copy-done.9) | copy-start | bytes 6291460
  1103.5 201.9 %all-to-all-start = ((bf16[8,128,1024]{1,2,0:T(8,128)(2,1)}), bf16[8,128,1024]{1,2,0:T(8,128)(2,1)}, u32[]{:S(2)}, u32[]{:S(2)}) async-start(bf16[8,128,1024]{1,2,0:T(8,128)(2,1)} %copy.73), calls=%async_computation.4 | async-start | bytes 4194304 | tf_op jit(solution)/shard_map/all_to_all | solution.py:23
  (6 other events, 5.8 us)
Sparse Core Ops, SparseCore 0:
  10.7 48.4 all-gather.10
  61.3 32.8 all-gather.8
  300.9 42.4 reduce-scatter.12
  345.6 49.2 all-gather.14
  397.0 32.9 all-gather.12
  432.2 49.2 all-gather.16
  483.1 32.9 all-gather.18
  539.0 44.5 reduce-scatter.16
  586.0 44.4 reduce-scatter.14
  637.7 34.4 all-gather.20
  1028.0 44.5 reduce-scatter.18
  1074.7 140.2 reduce-scatter.26
  1219.1 84.1 reduce-scatter.22
  1305.4 133.3 reduce-scatter.24
  1443.3 83.7 reduce-scatter.20
where the time goes:
time: 1540 us; the launch traced here: 1530 us
  waiting for transfers between devices  702 us (46%)
  local copies, waits for them, and re-layouts  291 us (19%)
  matrix products  275 us (18%)
  blocking collectives  118 us (8%)
  other arithmetic  106 us (7%)
  loops' own time  18.6 us (1%)
    unnamed x17, waiting for transfers between devices  232 us
    broadcast_in_dim x16, local copies, waits for them, and re-layouts, tile_scores(): scores = jnp.where(keep_mask, scores, NEGATIVE)  226 us
    reduce_scatter x4, waiting for transfers between devices, sum_rows(): lax.psum_scatter(partial_rows.astype(jnp.bfloat16), 'tensor', scatter_dim...  146 us
    all_gather x4, waiting for transfers between devices, gather_rows(): return lax.all_gather(local_rows, 'tensor', axis=0, tiled=True)  104 us
    reduce_scatter x1, waiting for transfers between devices, per_device(): lax.psum_scatter(grad_up, 'dp', scatter_dimension=0, tiled=True)  87 us
    reduce_scatter x1, waiting for transfers between devices, per_device(): lax.psum_scatter(grad_down, 'dp', scatter_dimension=0, tiled=True)  86.9 us
    dot_general x8, matrix products, tile_scores(): jnp.einsum('qhd,khd->hqk', query_tile, key_rows, preferred_element_type=j...  73.4 us
    convert_element_type x4, other arithmetic, one_tile(): (probabilities * (grad_probs - row_inner)).astype(jnp.bfloat16)  45.9 us
  transfers between devices with their start and end apart: 16, of which 13 were waited for; matrix products, arithmetic and copies ran while one was open for 6% of the time, Pallas kernels for 0%

commit v1 on v0

v1 whole, which is shorter than its diff:
```python
import functools

import jax
import jax.numpy as jnp
from jax import lax
from jax.experimental import pallas as pl
from jax.experimental.pallas import tpu as pltpu
from jax.sharding import PartitionSpec as P

HEAD_DIM = 64
BLOCK = 64
PAIR = 2 * HEAD_DIM
SLOTS = 8
CHUNK = 512
EPS = 1e-05
NEGATIVE = -1e30
F32 = jnp.float32
BF16 = jnp.bfloat16
NT = (((1,), (1,)), ((), ()))
NN = (((1,), (0,)), ((), ()))
TN = (((0,), (0,)), ((), ()))


def matmul(left, right, dims):
    return lax.dot_general(left, right, dims, preferred_element_type=F32)


def swapped(value, axis, bit):
    count = lax.axis_size(axis)
    return lax.ppermute(value, axis, [(i, i ^ bit) for i in range(count)])


def bits_of(axis):
    count = lax.axis_size(axis)
    return [1 << b for b in range(count.bit_length() - 1)]


def gathered_parts(value, axis):
    parts = {0: value}
    for bit in reversed(bits_of(axis)):
        parts.update({k | bit: swapped(p, axis, bit) for k, p in list(parts.items())})
    return [parts[k] for k in range(len(parts))]


def summed_part(parts, axis):
    left = dict(enumerate(parts))
    for bit in bits_of(axis):
        kept = {}
        for k in sorted(left, reverse=True):
            if k & bit == 0:
                arrived = swapped(left[k | bit].astype(BF16), axis, bit)
                kept[k] = left[k].astype(F32) + arrived.astype(F32)
        left = kept
    return left[0]


def exchanged_parts(parts, axis):
    return [p if k == 0 else swapped(p, axis, k) for k, p in enumerate(parts)]


def summed_everywhere(value, axes):
    size = value.shape[0]
    value = jnp.pad(value, (0, -size % 1024)).reshape(-1, 128)
    for axis in axes:
        for bit in bits_of(axis):
            value = value + swapped(value, axis, bit)
    return value.reshape(-1)[:size]


def sent_and_summed(value, axis):
    count = lax.axis_size(axis)
    blocks = value.reshape(count, value.shape[0] // count, *value.shape[1:])
    arrived = lax.all_to_all(blocks, axis, 0, 0, tiled=True)
    return jnp.sum(arrived.astype(F32), axis=0)


def attention_tables(length, place, chosen):
    count = place.shape[0]
    heads = chosen.shape[0]
    nblocks = (length + BLOCK - 1) // BLOCK
    last = nblocks - 1
    number = jnp.arange(count, dtype=jnp.int32)
    same = jnp.zeros_like(number)
    common = jnp.stack([same, same + last, number - 1, number, number + 1], axis=1)
    middle = (number > 0) & (number < last)
    good = jnp.stack(
        [
            middle | (number > last),
            middle | (number > last),
            (number - 1 > 0) & (number - 1 < last) & (number != last),
            middle,
            (number + 1 < last) & (number > 0),
        ],
        axis=1,
    )
    drawn = jnp.transpose(chosen, (1, 2, 0))
    away = number[:, None, None]
    fresh = (
        (drawn > 0)
        & (drawn < last)
        & (jnp.abs(drawn - away) > 1)
        & (away > 0)
        & (away != last)
    )
    first, second, third = drawn[:, 0], drawn[:, 1], drawn[:, 2]
    fresh = jnp.stack(
        [
            fresh[:, 0],
            fresh[:, 1] & (second != first),
            fresh[:, 2] & (third != first) & (third != second),
        ],
        axis=1,
    )
    flags = jnp.concatenate(
        [jnp.broadcast_to(good[:, :, None], (count, 5, heads)), fresh], axis=1
    )
    bias = jnp.where(flags, 0.0, NEGATIVE).astype(F32)
    bias = jnp.broadcast_to(bias[..., None], (*bias.shape, HEAD_DIM))
    bias = bias.reshape(count, SLOTS, heads * HEAD_DIM)
    wanted = jnp.concatenate([common, drawn.reshape(count, -1)], axis=1)
    hit = wanted[:, :, None] == place[None, None, :]
    stored = jnp.sum(jnp.where(hit, number[None, None, :], 0), axis=-1).astype(jnp.int32)
    limits = jnp.clip(length - BLOCK * place, 0, BLOCK).astype(jnp.int32)
    ends = jnp.stack([last, length - BLOCK * last]).astype(jnp.int32)
    return stored, limits, ends, bias


def block_rows(index):
    return pl.ds(pl.multiple_of(index * BLOCK, BLOCK), BLOCK)


def spread(rows, heads):
    lane = lax.broadcasted_iota(jnp.int32, (1, heads * HEAD_DIM), 1)
    zero = jnp.zeros_like(rows)
    return jnp.concatenate(
        [jnp.where(lane // HEAD_DIM == h, rows, zero) for h in range(heads)], axis=0
    )


def collapse(full, heads):
    lane = lax.broadcasted_iota(jnp.int32, (1, PAIR), 1)
    pieces = []
    for pair in range(heads // 2):
        cols = slice(PAIR * pair, PAIR * (pair + 1))
        even = full[2 * pair * HEAD_DIM : (2 * pair + 1) * HEAD_DIM, cols]
        odd = full[(2 * pair + 1) * HEAD_DIM : (2 * pair + 2) * HEAD_DIM, cols]
        pieces.append(jnp.where(lane < HEAD_DIM, even, odd))
    return jnp.concatenate(pieces, axis=1)


def gathered_keys(ref, start, stored, number, heads):
    width = heads * HEAD_DIM
    lane = lax.broadcasted_iota(jnp.int32, (1, PAIR), 1)
    parts = [ref[block_rows(stored[number, s]), start : start + width] for s in range(5)]
    for s in range(3):
        pieces = []
        for pair in range(heads // 2):
            cols = slice(start + PAIR * pair, start + PAIR * (pair + 1))
            at = 5 + heads * s + 2 * pair
            even = ref[block_rows(stored[number, at]), cols]
            odd = ref[block_rows(stored[number, at + 1]), cols]
            pieces.append(jnp.where(lane < HEAD_DIM, even, odd))
        parts.append(jnp.concatenate(pieces, axis=1))
    return jnp.concatenate(parts, axis=0)


def slot(value, index):
    return value[BLOCK * index : BLOCK * (index + 1)]


def biased(scores, bias, last_rows):
    row = lax.broadcasted_iota(jnp.int32, (BLOCK, 1), 0)
    parts = [slot(scores, s) + bias[s : s + 1] for s in range(SLOTS)]
    parts[1] = jnp.where(row < last_rows, parts[1], NEGATIVE)
    return parts


def total(parts):
    return functools.reduce(jnp.add, parts)


def attend_kernel(heads, stored, limits, ends, qkv_ref, bias_ref, out_ref, log_ref, keep_ref):
    count = bias_ref.shape[0]
    width = heads * HEAD_DIM
    scale = jnp.asarray(HEAD_DIM**-0.5, BF16)

    def item(number):
        here = block_rows(stored[number, 3])
        queries = spread(qkv_ref[here, :width] * scale, heads)
        keys = gathered_keys(qkv_ref, width, stored, number, heads)
        parts = biased(matmul(keys, queries, NT), bias_ref[number], ends[1])
        top = jnp.max(functools.reduce(jnp.maximum, parts), axis=0, keepdims=True)
        weights = [jnp.exp(p - top) for p in parts]
        row_total = jnp.sum(total(weights), axis=0, keepdims=True)
        inverse = 1.0 / row_total
        probs = jnp.concatenate([(p * inverse).astype(BF16) for p in weights], axis=0)
        values = gathered_keys(qkv_ref, 2 * width, stored, number, heads)
        out_ref[here, :] = collapse(matmul(probs, values, TN), heads).astype(BF16)
        log_ref[pl.ds(number, 1), :] = top + jnp.log(row_total)

    def step(number, carry):
        item(number)
        return carry

    lax.fori_loop(1, count, step, 0)

    row = lax.broadcasted_iota(jnp.int32, (BLOCK, 1), 0)
    per = CHUNK // BLOCK
    chunks = count // per

    def chunk_rows(chunk):
        return pl.ds(pl.multiple_of(chunk * CHUNK, CHUNK), CHUNK)

    for end in range(2):
        number = 0 if end == 0 else ends[0]
        here = block_rows(stored[number, 3])
        queries = spread(qkv_ref[here, :width] * scale, heads)

        def scores(chunk, top):
            at = chunk_rows(chunk)
            found = matmul(qkv_ref[at, width : 2 * width], queries, NT)
            parts = [
                jnp.where(row < limits[chunk * per + s], slot(found, s), NEGATIVE)
                for s in range(per)
            ]
            keep_ref[at, :] = jnp.concatenate(parts, axis=0)
            return jnp.maximum(top, functools.reduce(jnp.maximum, parts))

        top = lax.fori_loop(0, chunks, scores, jnp.full((BLOCK, width), NEGATIVE, F32))
        top = jnp.max(top, axis=0, keepdims=True)

        def exponents(chunk, row_total):
            at = chunk_rows(chunk)
            weights = jnp.exp(keep_ref[at, :] - top)
            keep_ref[at, :] = weights
            return row_total + total([slot(weights, s) for s in range(per)])

        row_total = lax.fori_loop(0, chunks, exponents, jnp.zeros((BLOCK, width), F32))
        row_total = jnp.sum(row_total, axis=0, keepdims=True)
        inverse = 1.0 / row_total

        def contexts(chunk, found):
            at = chunk_rows(chunk)
            probs = (keep_ref[at, :] * inverse).astype(BF16)
            return found + matmul(probs, qkv_ref[at, 2 * width :], TN)

        found = lax.fori_loop(0, chunks, contexts, jnp.zeros((width, width), F32))
        out_ref[here, :] = collapse(found, heads).astype(BF16)
        log_ref[pl.ds(number, 1), :] = top + jnp.log(row_total)


def attend_back_kernel(
    heads,
    stored,
    limits,
    ends,
    qkv_ref,
    grad_ref,
    bias_ref,
    log_ref,
    out_ref,
    keys_acc,
    values_acc,
    probs_ref,
    inner_ref,
):
    count = bias_ref.shape[0]
    width = heads * HEAD_DIM
    scale = jnp.asarray(HEAD_DIM**-0.5, BF16)
    lane = lax.broadcasted_iota(jnp.int32, (1, PAIR), 1)
    keys_acc[...] = jnp.zeros_like(keys_acc)
    values_acc[...] = jnp.zeros_like(values_acc)

    def accumulate(acc, value, number):
        for s in range(5):
            acc[block_rows(stored[number, s]), :] += slot(value, s)
        for s in range(3):
            for h in range(heads):
                cols = slice(PAIR * (h // 2), PAIR * (h // 2 + 1))
                mine = (lane < HEAD_DIM) == (h % 2 == 0)
                term = jnp.where(mine, slot(value, 5 + s)[:, cols], 0.0)
                acc[block_rows(stored[number, 5 + heads * s + h]), cols] += term

    def item(number):
        here = block_rows(stored[number, 3])
        queries = spread(qkv_ref[here, :width] * scale, heads)
        grads = spread(grad_ref[here, :], heads)
        keys = gathered_keys(qkv_ref, width, stored, number, heads)
        values = gathered_keys(qkv_ref, 2 * width, stored, number, heads)
        log_total = log_ref[pl.ds(number, 1), :]
        parts = biased(matmul(keys, queries, NT), bias_ref[number], ends[1])
        probs = [jnp.exp(p - log_total) for p in parts]
        found = matmul(values, grads, NT)
        found = [slot(found, s) for s in range(SLOTS)]
        inner = total([p * d for p, d in zip(probs, found)])
        inner = jnp.sum(inner, axis=0, keepdims=True)
        grad_scores = jnp.concatenate(
            [(p * (d - inner)).astype(BF16) for p, d in zip(probs, found)], axis=0
        )
        probs_low = jnp.concatenate([p.astype(BF16) for p in probs], axis=0)
        accumulate(values_acc, matmul(probs_low, grads, NN), number)
        accumulate(keys_acc, matmul(grad_scores, queries, NN), number)
        grad_queries = collapse(matmul(grad_scores, keys, TN), heads) * HEAD_DIM**-0.5
        out_ref[here, :width] = grad_queries.astype(BF16)

    def step(number, carry):
        item(number)
        return carry

    lax.fori_loop(1, count, step, 0)

    row = lax.broadcasted_iota(jnp.int32, (BLOCK, 1), 0)
    per = CHUNK // BLOCK
    chunks = count // per

    def chunk_rows(chunk):
        return pl.ds(pl.multiple_of(chunk * CHUNK, CHUNK), CHUNK)

    for end in range(2):
        number = 0 if end == 0 else ends[0]
        here = block_rows(stored[number, 3])
        queries = spread(qkv_ref[here, :width] * scale, heads)
        grads = spread(grad_ref[here, :], heads)
        log_total = log_ref[pl.ds(number, 1), :]

        def first(chunk, inner):
            at = chunk_rows(chunk)
            scores = matmul(qkv_ref[at, width : 2 * width], queries, NT)
            parts = [
                jnp.where(row < limits[chunk * per + s], slot(scores, s), NEGATIVE)
                for s in range(per)
            ]
            probs = jnp.exp(jnp.concatenate(parts, axis=0) - log_total)
            found = matmul(qkv_ref[at, 2 * width :], grads, NT)
            probs_ref[at, :] = probs
            inner_ref[at, :] = found
            both = probs * found
            return inner + total([slot(both, s) for s in range(per)])

        inner = lax.fori_loop(0, chunks, first, jnp.zeros((BLOCK, width), F32))
        inner = jnp.sum(inner, axis=0, keepdims=True)

        def second(chunk, grad_queries):
            at = chunk_rows(chunk)
            probs = probs_ref[at, :]
            grad_scores = (probs * (inner_ref[at, :] - inner)).astype(BF16)
            values_acc[at, :] += matmul(probs.astype(BF16), grads, NN)
            keys_acc[at, :] += matmul(grad_scores, queries, NN)
            return grad_queries + matmul(grad_scores, qkv_ref[at, width : 2 * width], TN)

        found = lax.fori_loop(0, chunks, second, jnp.zeros((width, width), F32))
        out_ref[here, :width] = (collapse(found, heads) * HEAD_DIM**-0.5).astype(BF16)

    out_ref[:, width : 2 * width] = keys_acc[...].astype(BF16)
    out_ref[:, 2 * width :] = values_acc[...].astype(BF16)


def in_smem():
    return pl.BlockSpec(memory_space=pltpu.SMEM)


def in_vmem():
    return pl.BlockSpec(memory_space=pltpu.VMEM)


def attention_cost(qkv, matmuls):
    rows, width = qkv.shape
    width //= 3
    return pl.CostEstimate(
        flops=2 * matmuls * rows * CHUNK * width,
        bytes_accessed=12 * rows * width,
        transcendentals=rows * CHUNK * width // HEAD_DIM,
    )


def attend(qkv, tables, heads):
    stored, limits, ends, bias = tables
    rows, width = qkv.shape[0], heads * HEAD_DIM
    return pl.pallas_call(
        functools.partial(attend_kernel, heads),
        out_shape=(
            jax.ShapeDtypeStruct((rows, width), BF16),
            jax.ShapeDtypeStruct((rows // BLOCK, width), F32),
        ),
        in_specs=[in_smem()] * 3 + [in_vmem()] * 2,
        out_specs=(in_vmem(), in_vmem()),
        scratch_shapes=[pltpu.VMEM((rows, width), F32)],
        compiler_params=pltpu.CompilerParams(vmem_limit_bytes=32 << 20),
        cost_estimate=attention_cost(qkv, 8),
        name="attend",
    )(stored, limits, ends, qkv, bias)


def attend_back(qkv, grad_context, log_totals, tables, heads):
    stored, limits, ends, bias = tables
    rows, width = qkv.shape[0], heads * HEAD_DIM
    return pl.pallas_call(
        functools.partial(attend_back_kernel, heads),
        out_shape=jax.ShapeDtypeStruct(qkv.shape, BF16),
        in_specs=[in_smem()] * 3 + [in_vmem()] * 4,
        out_specs=in_vmem(),
        scratch_shapes=[pltpu.VMEM((rows, width), F32)] * 4,
        compiler_params=pltpu.CompilerParams(vmem_limit_bytes=32 << 20),
        cost_estimate=attention_cost(qkv, 16),
        name="attend_back",
    )(stored, limits, ends, qkv, grad_context, bias, log_totals)


def unit_rows(rows):
    centred = rows - jnp.mean(rows, axis=-1, keepdims=True)
    inverse = lax.rsqrt(jnp.mean(centred * centred, axis=-1, keepdims=True) + EPS)
    return centred * inverse, inverse


def norm_back(grad_normed, unit, inverse, gain):
    grad_unit = grad_normed * gain
    return inverse * (
        grad_unit
        - jnp.mean(grad_unit, axis=-1, keepdims=True)
        - unit * jnp.mean(grad_unit * unit, axis=-1, keepdims=True)
    )


def gelu_tanh(pre_active):
    return jax.nn.gelu(pre_active, approximate=True)


def per_device(
    tokens,
    output_cotangent,
    lengths,
    block_place,
    random_blocks,
    qkv_weight,
    out_weight,
    up_weight,
    down_weight,
    vectors,
    hidden_bias,
):
    ways = lax.axis_size("tensor")
    spread_ways = lax.axis_size("dp")
    position = lax.axis_index("tensor")
    index = lax.axis_index("dp") * ways + position
    near = tokens.shape[0]
    rows = near * ways
    features = tokens.shape[1]
    width = qkv_weight.shape[2]
    heads = width // HEAD_DIM
    units = up_weight.shape[1]
    own = features // spread_ways
    piece = vectors.shape[1]
    unit_piece = hidden_bias.shape[1]

    def quarters(value):
        return [value[k * near : (k + 1) * near] for k in range(ways)]

    residual = tokens.astype(F32)
    unit_one, inverse_one = unit_rows(residual)
    unit_all = jnp.concatenate(gathered_parts(unit_one.astype(BF16), "tensor"), axis=0)

    qkv_flat = qkv_weight.reshape(own, 3 * width)
    qkv_full = lax.all_gather(qkv_flat, "dp", axis=0, tiled=True)
    out_group = lax.all_gather(out_weight, "dp", axis=0, tiled=True)
    up_full = lax.all_gather(up_weight, "dp", axis=0, tiled=True)
    down_full = lax.all_gather(down_weight, "dp", axis=0, tiled=True)

    small = jnp.zeros((8, features), F32)
    small = lax.dynamic_update_slice(small, vectors, (0, index * piece))
    small_hidden = jnp.zeros((1, units * ways), F32)
    small_hidden = lax.dynamic_update_slice(small_hidden, hidden_bias, (0, index * unit_piece))
    packed = jnp.concatenate([small.reshape(-1), small_hidden.reshape(-1)])
    packed = summed_everywhere(packed, ("tensor", "dp"))
    vectors_full = packed[: 8 * features].reshape(8, features)
    hidden_full = packed[8 * features :]
    bias_query = lax.dynamic_slice_in_dim(vectors_full[6], position * width, width)
    bias_value = lax.dynamic_slice_in_dim(vectors_full[7], position * width, width)
    bias_qkv = jnp.concatenate([bias_query, jnp.zeros_like(bias_query), bias_value])
    bias_hidden = lax.dynamic_slice_in_dim(hidden_full, position * units, units)

    placed = block_place[0].reshape(ways, -1)
    order = position ^ jnp.arange(ways, dtype=jnp.int32)
    chosen_rows = order[:, None, None] == jnp.arange(ways, dtype=jnp.int32)[None, :, None]
    place = jnp.sum(jnp.where(chosen_rows, placed[None], 0), axis=1).reshape(-1)
    tables = attention_tables(lengths[0], place, random_blocks[0])

    normed_one_all = (unit_all.astype(F32) * vectors_full[0] + vectors_full[1]).astype(BF16)
    qkv = (matmul(normed_one_all, qkv_full, NN) + bias_qkv).astype(BF16)
    context, log_totals = attend(qkv, tables, heads)

    out_all = jnp.concatenate(gathered_parts(out_group, "tensor"), axis=1)
    context_near = jnp.concatenate(exchanged_parts(quarters(context), "tensor"), axis=1)
    middle = residual + matmul(context_near, out_all, NT) + vectors_full[4]
    unit_two, inverse_two = unit_rows(middle)
    normed_two = (unit_two * vectors_full[2] + vectors_full[3]).astype(BF16)
    normed_two_all = jnp.concatenate(gathered_parts(normed_two, "tensor"), axis=0)
    grad_all = jnp.concatenate(gathered_parts(output_cotangent, "tensor"), axis=0)

    hidden = matmul(normed_two_all, up_full, NN) + bias_hidden
    active, gelu_pullback = jax.vjp(gelu_tanh, hidden)
    active = active.astype(BF16)
    grad_hidden = gelu_pullback(matmul(grad_all, down_full, NN))[0].astype(BF16)
    grad_normed_two = summed_part(quarters(matmul(grad_hidden, up_full, NT)), "tensor")
    feed_out = summed_part(quarters(matmul(active, down_full, NT)), "tensor")
    output = (middle + feed_out + vectors_full[5]).astype(BF16)
    up_weight_grad = sent_and_summed(matmul(normed_two_all, grad_hidden, TN).astype(BF16), "dp")
    down_weight_grad = sent_and_summed(matmul(grad_all, active, TN).astype(BF16), "dp")
    sum_hidden = jnp.sum(grad_hidden, axis=0, dtype=F32)

    cotangent = output_cotangent.astype(F32)
    grad_middle = cotangent + norm_back(grad_normed_two, unit_two, inverse_two, vectors_full[2])
    grad_attended = grad_middle.astype(BF16)
    grad_heads = matmul(grad_attended, out_all, NN).astype(BF16)
    grad_heads = [grad_heads[:, k * width : (k + 1) * width] for k in range(ways)]
    grad_context = jnp.concatenate(exchanged_parts(grad_heads, "tensor"), axis=0)
    grad_qkv = attend_back(qkv, grad_context, log_totals, tables, heads)

    raw_qkv = matmul(unit_all, grad_qkv, TN)
    sum_qkv = jnp.sum(grad_qkv, axis=0, dtype=F32)
    qkv_wide = qkv_full.astype(F32)
    gain_one = jnp.sum(raw_qkv * qkv_wide, axis=1)
    shift_one = jnp.sum(sum_qkv * qkv_wide, axis=1)
    grad_normed_one = summed_part(quarters(matmul(grad_qkv, qkv_full, NT)), "tensor")
    out_grad = matmul(grad_attended, context_near, TN)
    out_grad = [out_grad[:, k * width : (k + 1) * width] for k in range(ways)]
    out_grad = summed_part(out_grad, "tensor").astype(BF16)
    sent = jnp.concatenate([raw_qkv.astype(BF16), out_grad], axis=1)
    arrived = sent_and_summed(sent, "dp")

    input_grad = (
        grad_middle + norm_back(grad_normed_one, unit_one, inverse_one, vectors_full[0])
    ).astype(BF16)

    by_feature = jnp.stack(
        [
            gain_one,
            shift_one,
            jnp.sum(grad_normed_two * unit_two, axis=0),
            jnp.sum(grad_normed_two, axis=0),
            jnp.sum(grad_middle, axis=0),
            jnp.sum(cotangent, axis=0),
        ]
    )
    by_feature = jnp.transpose(by_feature.reshape(6, spread_ways, own), (1, 0, 2))
    by_head = jnp.concatenate([sum_qkv, sum_hidden])
    by_head = jnp.broadcast_to(by_head[None], (spread_ways, by_head.shape[0]))
    extras = jnp.concatenate([by_feature.reshape(spread_ways, -1), by_head], axis=1)
    extras = jnp.sum(lax.all_to_all(extras, "dp", 0, 0, tiled=True), axis=0)
    sum_qkv = extras[6 * own : 6 * own + 3 * width]
    sum_hidden = extras[6 * own + 3 * width :]
    head_sums = jnp.zeros((2, features), F32)
    head_sums = lax.dynamic_update_slice(
        head_sums,
        jnp.stack([sum_qkv[:width], sum_qkv[2 * width :]]),
        (0, position * width),
    )
    hidden_sums = lax.dynamic_update_slice(
        jnp.zeros((units * ways,), F32), sum_hidden, (position * units,)
    )
    packed = jnp.concatenate([extras[: 6 * own], head_sums.reshape(-1), hidden_sums])
    packed = summed_everywhere(packed, ("tensor",))
    by_feature = packed[: 6 * own].reshape(6, own)
    head_sums = packed[6 * own : 6 * own + 2 * features].reshape(2, features)
    hidden_sums = packed[6 * own + 2 * features :]
    vectors_grad = jnp.concatenate(
        [
            lax.dynamic_slice_in_dim(by_feature, position * piece, piece, axis=1),
            lax.dynamic_slice_in_dim(head_sums, index * piece, piece, axis=1),
        ],
        axis=0,
    )
    hidden_bias_grad = lax.dynamic_slice_in_dim(hidden_sums, index * unit_piece, unit_piece)

    mine = lax.dynamic_slice_in_dim(
        vectors_full[:2], lax.axis_index("dp") * own, own, axis=1
    )
    qkv_weight_grad = mine[0][:, None] * arrived[:, : 3 * width] + mine[1][:, None] * sum_qkv
    return (
        output,
        input_grad,
        qkv_weight_grad.reshape(own, 3, width),
        arrived[:, 3 * width :],
        up_weight_grad,
        down_weight_grad,
        vectors_grad,
        hidden_bias_grad[None, :],
    )


def solution(mesh):
    placed = (
        P(("dp", "tensor"), None),
        P(("dp", "tensor"), None),
        P("dp"),
        P("dp", None),
        P("dp", "tensor", None, None),
        P("dp", None, "tensor"),
        P("dp", "tensor"),
        P("dp", "tensor"),
        P("dp", "tensor"),
        P(None, ("dp", "tensor")),
        P(None, ("dp", "tensor")),
    )
    return jax.shard_map(
        per_device,
        mesh=mesh,
        in_specs=placed,
        out_specs=(
            P(("dp", "tensor"), None),
            P(("dp", "tensor"), None),
            P("dp", None, "tensor"),
            P("dp", "tensor"),
            P("dp", "tensor"),
            P("dp", "tensor"),
            P(None, ("dp", "tensor")),
            P(None, ("dp", "tensor")),
        ),
        check_vma=False,
    )
```

time: 1540 us -> 524 us (0.34)
  waiting for transfers between devices: 702 us -> 223 us
  local copies, waits for them, and re-layouts: 291 us -> 25.2 us
  matrix products: 275 us -> 83.4 us
  blocking collectives: 118 us -> 33.8 us
  other arithmetic: 106 us -> 30.9 us
  Pallas kernels: 0 us -> 60.8 us
  starting transfers between devices: 7.06 us -> 42.8 us
  loops' own time: 18.6 us -> 0 us
    reduce_scatter x6 -> x0, waiting for transfers between devices: 320 us -> none  [the longest x4 146 us: sum_rows(): lax.psum_scatter(partial_rows.astype(jnp.bfloat16), 'tensor', scatter_dim...]
    unnamed x17 -> x3, waiting for transfers between devices: 232 us -> 0.73 us
    broadcast_in_dim x18 -> x9, local copies, waits for them, and re-layouts: 226 us -> 1.02 us  [the longest x1 0.58 us: per_device(): hidden_bias_grad[None, :]]
    dot_general x40 -> x12, matrix products: 275 us -> 83.4 us  [matmul(): return lax.dot_general(left, right, dims, preferred_element_type=F32)]
    ppermute x0 -> x37, waiting for transfers between devices: none -> 159 us  [swapped(): return lax.ppermute(value, axis, [(i, i ^ bit) for i in range(count)])]
    all_gather x7 -> x3, waiting for transfers between devices: 150 us -> 0.02 us  [the longest x1 0.02 us: per_device(): qkv_full = lax.all_gather(qkv_flat, 'dp', axis=0, tiled=True)]
    all_gather x3 -> x1, blocking collectives: 118 us -> 33.8 us  [per_device(): out_group = lax.all_gather(out_weight, 'dp', axis=0, tiled=True)]
    all_to_all x1 -> x4, waiting for transfers between devices: 0.01 us -> 64 us  [the longest x3 64 us: sent_and_summed(): arrived = lax.all_to_all(blocks, axis, 0, 0, tiled=True)]
  transfers between devices with their start and end apart: 16 -> 44, of which waited for: 13 -> 19; matrix products, arithmetic and copies ran while one was open for 6% -> 20% of each run, Pallas kernels for 0% -> 5%
where the time goes in v1:
time: 524 us; the launch traced here: 516 us
  waiting for transfers between devices  223 us (43%)
  matrix products  83.4 us (16%)
  Pallas kernels  60.8 us (12%)
  starting transfers between devices  42.8 us (8%)
  blocking collectives  33.8 us (6%)
  other arithmetic  30.9 us (6%)
  local copies, waits for them, and re-layouts  25.2 us (5%)
  between operations  15.9 us (3%)
    ppermute x37, waiting for transfers between devices, swapped(): return lax.ppermute(value, axis, [(i, i ^ bit) for i in range(count)])  159 us
    dot_general x12, matrix products, matmul(): return lax.dot_general(left, right, dims, preferred_element_type=F32)  83.4 us
    all_to_all x3, waiting for transfers between devices, sent_and_summed(): arrived = lax.all_to_all(blocks, axis, 0, 0, tiled=True)  64 us
    all_gather x1, blocking collectives, per_device(): out_group = lax.all_gather(out_weight, 'dp', axis=0, tiled=True)  33.8 us
    pallas_call x1, Pallas kernels, attend_back(): pl.pallas_call(functools.partial(attend_back_kernel, heads), out_shape=ja...  32.5 us
    pallas_call x1, Pallas kernels, attend(): pl.pallas_call(functools.partial(attend_kernel, heads), out_shape=(jax.Sh...  28.3 us
    ppermute x37, starting transfers between devices, swapped(): return lax.ppermute(value, axis, [(i, i ^ bit) for i in range(count)])  22.2 us
    unnamed x80, local copies, waits for them, and re-layouts  16 us
  transfers between devices with their start and end apart: 44, of which 19 were waited for; matrix products, arithmetic and copies ran while one was open for 20% of the time, Pallas kernels for 5%

profile of v1, /device:TPU:0, one launch (start us, length us, event | category | flops | bytes accessed | tf_op | source)
XLA Modules:
  0.0 516.3 jit_solution(12930028508975454437)
XLA Ops:
  7.3 1.8 copy.65
  9.9 33.8 %all_gather.13 = bf16[1024,256]{1,0:T(8,128)(2,1)S(1)} all-gather(bf16[128,256]{1,0:T(8,128)(2,1)} %param.17), channel_id=1, replica_groups=mesh['dp'=8,'tensor'=4] {'dp'}, dimensions={0}, use_global_device_ids=true | all-gather | bytes 589824 | tf_op jit(solution)/shard_map/all_gather | solution.py:464
  43.7 1.6 collective-permute-start.12
  45.3 1.4 convert_reduce_fusion.5
  52.9 22.6 %collective-permute-done.1 = bf16[512,1024]{1,0:T(8,128)(2,1)} collective-permute-done((bf16[512,1024]{1,0:T(8,128)(2,1)S(1)}, bf16[512,1024]{1,0:T(8,128)(2,1)}, u32[]{:S(2)}, u32[]{:S(2)}) %collective-permute-start.1) | collective-permute-done | bytes 1048608 | tf_op jit(solution)/shard_map/ppermute | solution.py:30
  75.5 1.6 collective-permute-start.4
  77.1 2.6 collective-permute-done.4
  79.7 1.5 collective-permute-start.5
  81.3 2.6 collective-permute-done.5
  84.0 4.0 collective-permute-done.6
  88.1 1.4 collective-permute-start.7
  90.4 5.5 %collective-permute-done.7 = f32[96,128]{1,0:T(8,128)S(1)} collective-permute-done((f32[96,128]{1,0:T(8,128)S(1)}, f32[96,128]{1,0:T(8,128)S(1)}, u32[]{:S(2)}, u32[]{:S(2)}) %collective-permute-start.7) | collective-permute-done | bytes 49184 | tf_op jit(solution)/shard_map/ppermute | solution.py:30
  96.6 1.5 collective-permute-start.21
  99.2 6.0 %add_convert_fusion.1.qkv_ref = bf16[2048,768]{1,0:T(8,128)(2,1)S(1)} fusion(f32[768]{0:T(1024)S(1)} %pad_maximum_fusion.12, bf16[1024,768]{0,1:T(8,128)(2,1)} %all-gather.4.cloned.1.call-done, f32[1024]{0:T(1024)S(1)} %get-tuple-element.83, f32[1024]{0:T(1024)S(1)} %get-tuple-element.84, bf16[512,1024]{1,0:T(8,128)(2,1)} %collective-permute-done.2, ...), kind=kOutput, calls=%fused_computation.13 | convolution fusion | flops 3247439872 | bytes 8924160 | tf_op jit(solution)/shard_map/dot_general | solution.py:25
  105.3 28.3 %attend.1 = (bf16[2048,256]{1,0:T(8,128)(2,1)S(1)}, f32[32,256]{1,0:T(8,128)S(1)}) custom-call(s32[32,17]{1,0:T(8,128)S(1)} %copy.67.stored, s32[32]{0:T(128)S(1)} %subtract_clamp_fusion.limits, s32[2]{0:T(128)S(1)} %pad_add_fusion.ends, bf16[2048,768]{1,0:T(8,128)(2,1)S(1)} %add_convert_fusion.1.qkv_ref, f32[32,8,256]{2,1,0:T(8,128)S(1)} %reshape.293.bias_ref), custom_call_target="tpu_custom_call" | custom-call | flops 4294967296 | bytes 6291456 | tf_op jit(solution)/shard_map/attend/pallas_call | solution.py:379
  134.3 1.5 collective-permute-start.9
  138.1 3.6 collective-permute-done.10
  141.7 6.2 %collective-permute-done.9 = bf16[512,256]{1,0:T(8,128)(2,1)S(1)} collective-permute-done((bf16[512,256]{1,0:T(8,128)(2,1)S(1)}, bf16[512,256]{1,0:T(8,128)(2,1)S(1)}, u32[]{:S(2)}, u32[]{:S(2)}) %collective-permute-start.9) | collective-permute-done | bytes 262176 | tf_op jit(solution)/shard_map/ppermute | solution.py:30
  147.9 1.4 fusion.68
  151.3 23.8 %collective-permute-done.15 = bf16[512,1024]{1,0:T(8,128)(2,1)} collective-permute-done((bf16[512,1024]{1,0:T(8,128)(2,1)S(1)}, bf16[512,1024]{1,0:T(8,128)(2,1)}, u32[]{:S(2)}, u32[]{:S(2)}) %collective-permute-start.15) | collective-permute-done | bytes 1048608 | tf_op jit(solution)/shard_map/ppermute | solution.py:30
  175.1 2.4 constant_dynamic-update-slice_fusion.7
  177.4 2.3 constant_dynamic-update-slice_fusion.6
  179.7 2.3 constant_dynamic-update-slice_fusion.5
  182.0 2.3 constant_dynamic-update-slice_fusion.4
  184.3 10.4 %fusion.37 = f32[2048,1024]{1,0:T(8,128)} fusion(bf16[1024,1024]{1,0:T(8,128)(2,1)} %all-gather.6.cloned.1.call-done, bf16[512,1024]{1,0:T(8,128)(2,1)} %collective-permute-done.16, bf16[512,1024]{1,0:T(8,128)(2,1)} %collective-permute-done.15, bf16[512,1024]{1,0:T(8,128)(2,1)} %collective-permute-done.14, bf16[512,1024]{1,0:T(8,128)(2,1)S(1)} %add_convert_fusion.5), kind=kOutput, calls=%fused_computation.77 | convolution fusion | flops 4311744512 | bytes 14680064 | tf_op jit(solution)/shard_map/dot_general | solution.py:25
  194.7 13.9 %convert_reduce_fusion = (f32[1024]{0:T(1024)S(1)}, bf16[2048,1024]{1,0:T(8,128)(2,1)S(1)}) fusion(f32[2048,1024]{1,0:T(8,128)} %fusion.37, f32[1024]{0:T(1024)S(1)} %dynamic_slice.23, bf16[2048,1024]{1,0:T(8,128)(2,1)} %constant_dynamic-update-slice_fusion.4, bf16[1024,1024]{1,0:T(8,128)(2,1)} %all-gather.8.cloned.1.call-done), kind=kOutput, calls=%fused_computation.9 | convolution fusion | flops 4343200768 | bytes 18882560 | tf_op jit(solution)/shard_map/dot_general | solution.py:25
  208.6 4.7 fusion.69
  214.9 8.5 %fusion.70 = (bf16[2048,1024]{1,0:T(8,128)(2,1)S(1)}, f32[2048,1024]{1,0:T(8,128)S(1)}) fusion(bf16[1024,1024]{1,0:T(8,128)(2,1)} %all-gather.8.cloned.1.call-done, f32[2048,1024]{1,0:T(8,128)} %fusion.37, f32[1024]{0:T(1024)S(1)} %dynamic_slice.23), kind=kOutput, calls=%fused_computation.179 | convolution fusion | flops 4318035968 | bytes 23072768 | tf_op jit(solution)/shard_map/dot_general | solution.py:25
  224.2 1.6 fusion.27
  226.7 1.6 collective-permute-start.19
  228.3 23.6 %collective-permute-done.25 = bf16[512,1024]{1,0:T(8,128)(2,1)S(1)} collective-permute-done((bf16[512,1024]{1,0:T(8,128)(2,1)S(1)}, bf16[512,1024]{1,0:T(8,128)(2,1)S(1)}, u32[]{:S(2)}, u32[]{:S(2)}) %collective-permute-start.25) | collective-permute-done | bytes 1048608 | tf_op jit(solution)/shard_map/ppermute | solution.py:30
  251.9 1.2 multiply_reduce_fusion
  253.1 20.3 %collective-permute-done.19 = bf16[512,1024]{1,0:T(8,128)(2,1)S(1)} collective-permute-done((bf16[512,1024]{1,0:T(8,128)(2,1)S(1)}, bf16[512,1024]{1,0:T(8,128)(2,1)S(1)}, u32[]{:S(2)}, u32[]{:S(2)}) %collective-permute-start.19) | collective-permute-done | bytes 1048608 | tf_op jit(solution)/shard_map/ppermute | solution.py:30
  273.5 3.4 fusion.57
  276.9 1.3 convolution_convert_fusion.2
  280.2 6.7 %collective-permute-done.28 = bf16[512,256]{1,0:T(8,128)(2,1)S(1)} collective-permute-done((bf16[512,256]{1,0:T(8,128)(2,1)S(1)}, bf16[512,256]{1,0:T(8,128)(2,1)S(1)}, u32[]{:S(2)}, u32[]{:S(2)}) %collective-permute-start.28) | collective-permute-done | bytes 262176 | tf_op jit(solution)/shard_map/ppermute | solution.py:30
  286.9 4.6 collective-permute-done.27
  291.5 32.5 %attend_back.1 = bf16[2048,768]{1,0:T(8,128)(2,1)S(1)} custom-call(s32[32,17]{1,0:T(8,128)S(1)} %copy.67.stored, s32[32]{0:T(128)S(1)} %subtract_clamp_fusion.limits, s32[2]{0:T(128)S(1)} %pad_add_fusion.ends, bf16[2048,768]{1,0:T(8,128)(2,1)S(1)} %copy-done.1, bf16[2048,256]{1,0:T(8,128)(2,1)S(1)} %pad_maximum_fusion.3.grad_ref, ...), custom_call_target="tpu_custom_call" | custom-call | flops 8589934592 | bytes 6291456 | tf_op jit(solution)/shard_map/attend_back/pallas_call | solution.py:397
  325.8 6.3 %fusion.11 = (f32[1024]{0:T(1024)S(1)}, f32[1024]{0:T(1024)S(1)}, bf16[1024,768]{0,1:T(8,128)(2,1)}) fusion(bf16[1024,768]{0,1:T(8,128)(2,1)S(1)} %copy-done.26, f32[768]{0:T(1024)S(1)} %convert_reduce_fusion.1, bf16[2048,768]{1,0:T(8,128)(2,1)S(1)} %attend_back.1, bf16[512,1024]{1,0:T(8,128)(2,1)} %collective-permute-done.2, ...), kind=kOutput, calls=%fused_computation.25 | convolution fusion | flops 3242719232 | bytes 10497024 | tf_op jit(solution)/shard_map/dot_general | solution.py:25
  332.8 5.9 %all-to-all-start.1 = ((f32[8,1,2560]{2,1,0:T(1,128)}), f32[8,1,2560]{2,1,0:T(1,128)S(1)}, u32[]{:S(2)}, u32[]{:S(2)}) async-start(f32[8,1,2560]{2,1,0:T(1,128)} %all_to_all.16), calls=%async_computation.1 | async-start | bytes 163840 | tf_op jit(solution)/shard_map/all_to_all | solution.py:548
  338.7 9.4 %convolution_convert_fusion.1 = bf16[1024,1024]{1,0:T(8,128)(2,1)} fusion(bf16[2048,1024]{1,0:T(8,128)(2,1)} %copy-done.30, bf16[512,1024]{1,0:T(8,128)(2,1)} %collective-permute-done.16, bf16[512,1024]{1,0:T(8,128)(2,1)} %collective-permute-done.15, bf16[512,1024]{1,0:T(8,128)(2,1)} %collective-permute-done.14, bf16[512,1024]{1,0:T(8,128)(2,1)} %copy-done.9), kind=kOutput, calls=%fused_computation.67 | convolution fusion | flops 4312793088 | bytes 10485760 | tf_op jit(solution)/shard_map/dot_general | solution.py:25
  348.1 6.3 %all-to-all-start.2 = ((bf16[8,128,1024]{2,1,0:T(8,128)(2,1)}), bf16[8,128,1024]{2,1,0:T(8,128)(2,1)}, u32[]{:S(2)}, u32[]{:S(2)}) async-start(bf16[8,128,1024]{2,1,0:T(8,128)(2,1)} %bitcast.105), calls=%async_computation.2 | async-start | bytes 4194304 | tf_op jit(solution)/shard_map/all_to_all | solution.py:73
  354.4 11.0 %convolution_convert_fusion = bf16[1024,1024]{1,0:T(8,128)(2,1)} fusion(bf16[2048,1024]{1,0:T(8,128)(2,1)} %constant_dynamic-update-slice_fusion.4, f32[2048,1024]{1,0:T(8,128)} %fusion.37, f32[1024]{0:T(1024)S(1)} %dynamic_slice.23), kind=kOutput, calls=%fused_computation.66 | convolution fusion | flops 4316987392 | bytes 14684160 | tf_op jit(solution)/shard_map/dot_general | solution.py:25
  365.4 37.2 %all-to-all-done.2 = bf16[8,128,1024]{2,1,0:T(8,128)(2,1)} async-done(((bf16[8,128,1024]{2,1,0:T(8,128)(2,1)}), bf16[8,128,1024]{2,1,0:T(8,128)(2,1)}, u32[]{:S(2)}, u32[]{:S(2)}) %all-to-all-start.2) | async-done | bytes 2097184 | tf_op jit(solution)/shard_map/all_to_all | solution.py:73
  402.6 4.4 all-to-all-start.3
  407.0 5.1 fusion.72
  413.7 5.6 %fusion.71 = (bf16[2048,1024]{1,0:T(8,128)(2,1)S(1)}, f32[2048,1024]{1,0:T(8,128)}) fusion(bf16[2048,768]{1,0:T(8,128)(2,1)S(1)} %attend_back.1, bf16[1024,768]{0,1:T(8,128)(2,1)S(1)} %copy-done.27), kind=kOutput, calls=%fused_computation.180 | convolution fusion | flops 3223322624 | bytes 17301504 | tf_op jit(solution)/shard_map/dot_general | solution.py:25
  420.5 1.6 fusion.34
  422.1 1.5 collective-permute-start.34
  423.6 12.8 %collective-permute-done.34 = bf16[1024,256]{0,1:T(8,128)(2,1)S(1)} collective-permute-done((bf16[1024,256]{0,1:T(8,128)(2,1)S(1)}, bf16[1024,256]{0,1:T(8,128)(2,1)S(1)}, u32[]{:S(2)}, u32[]{:S(2)}) %collective-permute-start.34) | collective-permute-done | bytes 524320 | tf_op jit(solution)/shard_map/ppermute | solution.py:30
  436.4 1.6 fusion.36
  438.0 1.8 copy_bitcast_fusion
  439.8 15.0 %all-to-all-done.3 = bf16[8,128,1024]{2,1,0:T(8,128)(2,1)} async-done(((bf16[8,128,1024]{2,1,0:T(8,128)(2,1)}), bf16[8,128,1024]{2,1,0:T(8,128)(2,1)}, u32[]{:S(2)}, u32[]{:S(2)}) %all-to-all-start.3) | async-done | bytes 2097184 | tf_op jit(solution)/shard_map/all_to_all | solution.py:73
  454.8 3.9 all-to-all-start
  460.1 1.5 collective-permute-start.36
  461.5 2.5 collective-permute-done.36
  464.1 2.2 fusion.24
  466.3 1.5 collective-permute-start.31
  469.1 2.8 convert_reduce_fusion.3
  471.9 2.8 convert_reduce_fusion.2
  474.7 16.1 %collective-permute-done.31 = bf16[512,1024]{1,0:T(8,128)(2,1)S(1)} collective-permute-done((bf16[512,1024]{1,0:T(8,128)(2,1)S(1)}, bf16[512,1024]{1,0:T(8,128)(2,1)S(1)}, u32[]{:S(2)}, u32[]{:S(2)}) %collective-permute-start.31) | collective-permute-done | bytes 1048608 | tf_op jit(solution)/shard_map/ppermute | solution.py:30
  490.8 2.9 fusion.55
  493.7 1.7 fusion.21
  495.3 11.8 %all-to-all-done = bf16[8,128,1024]{1,2,0:T(8,128)(2,1)S(1)} async-done(((bf16[8,128,1024]{1,2,0:T(8,128)(2,1)}), bf16[8,128,1024]{1,2,0:T(8,128)(2,1)S(1)}, u32[]{:S(2)}, u32[]{:S(2)}) %all-to-all-start) | async-done | bytes 2097184 | tf_op jit(solution)/shard_map/all_to_all | solution.py:73
  (230 shorter events, 29.4 us)
Async XLA Ops:
  7.2 39.6 %copy-start.2 = (bf16[512,1024]{1,0:T(8,128)(2,1)S(1)}, bf16[512,1024]{1,0:T(8,128)(2,1)}, u32[]{:S(2)}) copy-start(bf16[512,1024]{1,0:T(8,128)(2,1)} %param.11) | copy-start | bytes 3145732
  7.2 41.1 %copy-start.24 = (f32[8,32]{1,0:T(8,128)S(1)}, f32[8,32]{1,0:T(8,128)}, u32[]{:S(2)}) copy-start(f32[8,32]{1,0:T(8,128)} %param.20) | copy-start | bytes 3076
  7.2 41.3 %copy-start.28 = (f32[1,128]{1,0:T(1,128)S(1)}, f32[1,128]{1,0:T(1,128)}, u32[]{:S(2)}) copy-start(f32[1,128]{1,0:T(1,128)} %param.21) | copy-start | bytes 1540
  7.2 42.5 %copy-start.29 = (s32[1,32]{1,0:T(1,128)S(1)}, s32[1,32]{1,0:T(1,128)}, u32[]{:S(2)}) copy-start(s32[1,32]{1,0:T(1,128)} %param.14) | copy-start | bytes 388
  7.2 44.1 %copy-start.18 = (s32[1,4,32,3]{2,1,3,0:T(4,128)S(1)}, s32[1,4,32,3]{2,1,3,0:T(4,128)}, u32[]{:S(2)}) copy-start(s32[1,4,32,3]{2,1,3,0:T(4,128)} %param.15) | copy-start | bytes 4612
  7.2 92.0 %all-gather.4.cloned.1.call-start = ((), (), s32[]{:S(2)}) async-start(), calls=%async_computation.4 | async-start | bytes 1769472 | tf_op jit(solution)/shard_map/all_gather | solution.py:463
  9.1 175.2 %all-gather.6.cloned.1.call-start = ((), (), s32[]{:S(2)}) async-start(), calls=%async_computation.5 | async-start | bytes 2359296 | tf_op jit(solution)/shard_map/all_gather | solution.py:465
  9.9 184.8 %all-gather.8.cloned.1.call-start = ((), (), s32[]{:S(2)}) async-start(), calls=%async_computation.6 | async-start | bytes 2359296 | tf_op jit(solution)/shard_map/all_gather | solution.py:466
  43.7 55.4 %collective-permute-start.12 = (bf16[1024,256]{1,0:T(8,128)(2,1)S(1)}, bf16[1024,256]{1,0:T(8,128)(2,1)}, u32[]{:S(2)}, u32[]{:S(2)}) collective-permute-start(bf16[1024,256]{1,0:T(8,128)(2,1)S(1)} %all_gather.13), channel_id=1, source_target_pairs={{0,2},{1,3},{2,0},{3,1},{4,6},{5,7},{6,4},{7,5},{8,10},{9,11},{10,... | collective-permute-start | bytes 1572872 | tf_op jit(solution)/shard_map/ppermute | solution.py:30
  45.3 90.5 %collective-permute-start.11 = (bf16[1024,256]{1,0:T(8,128)(2,1)S(1)}, bf16[1024,256]{1,0:T(8,128)(2,1)}, u32[]{:S(2)}, u32[]{:S(2)}) collective-permute-start(bf16[1024,256]{1,0:T(8,128)(2,1)S(1)} %all_gather.13), channel_id=1, source_target_pairs={{0,1},{1,0},{2,3},{3,2},{4,5},{5,4},{6,7},{7,6},{8,9},{9,8},{10,11... | collective-permute-start | bytes 1572872 | tf_op jit(solution)/shard_map/ppermute | solution.py:30
  47.5 57.7 %copy-start.7 = (bf16[512,1024]{1,0:T(8,128)(2,1)}, bf16[512,1024]{1,0:T(8,128)(2,1)S(1)}, u32[]{:S(2)}) copy-start(bf16[512,1024]{1,0:T(8,128)(2,1)S(1)} %fusion.16) | copy-start | bytes 3145732
  47.5 28.0 %collective-permute-start.1 = (bf16[512,1024]{1,0:T(8,128)(2,1)S(1)}, bf16[512,1024]{1,0:T(8,128)(2,1)}, u32[]{:S(2)}, u32[]{:S(2)}) collective-permute-start(bf16[512,1024]{1,0:T(8,128)(2,1)S(1)} %fusion.16), channel_id=1, source_target_pairs={{0,2},{1,3},{2,0},{3,1},{4,6},{5,7},{6,4},{7,5},{8,10},{9,11},{10,... | collective-permute-start | bytes 3145736 | tf_op jit(solution)/shard_map/ppermute | solution.py:30
  48.0 51.1 %collective-permute-start = (bf16[512,1024]{1,0:T(8,128)(2,1)S(1)}, bf16[512,1024]{1,0:T(8,128)(2,1)}, u32[]{:S(2)}, u32[]{:S(2)}) collective-permute-start(bf16[512,1024]{1,0:T(8,128)(2,1)S(1)} %fusion.16), channel_id=1, source_target_pairs={{0,1},{1,0},{2,3},{3,2},{4,5},{5,4},{6,7},{7,6},{8,9},{9,8},{10,11... | collective-permute-start | bytes 3145736 | tf_op jit(solution)/shard_map/ppermute | solution.py:30
  48.7 26.8 %collective-permute-start.3 = (f32[96,128]{1,0:T(8,128)S(1)}, f32[96,128]{1,0:T(8,128)S(1)}, u32[]{:S(2)}, u32[]{:S(2)}) collective-permute-start(f32[96,128]{1,0:T(8,128)S(1)} %maximum_bitcast_fusion.1), channel_id=1, source_target_pairs={{0,1},{1,0},{2,3},{3,2},{4,5},{5,4},{6,7},{7,6},{8,9},{9,8},{10,11... | collective-permute-start | bytes 147464 | tf_op jit(solution)/shard_map/ppermute | solution.py:30
  75.5 23.7 %collective-permute-start.2 = (bf16[512,1024]{1,0:T(8,128)(2,1)}, bf16[512,1024]{1,0:T(8,128)(2,1)}, u32[]{:S(2)}, u32[]{:S(2)}) collective-permute-start(bf16[512,1024]{1,0:T(8,128)(2,1)} %collective-permute-done.1), channel_id=1, source_target_pairs={{0,1},{1,0},{2,3},{3,2},{4,5},{5,4},{6,7},{7,6},{8,9},{9,8},{10,11... | collective-permute-start | bytes 3145736 | tf_op jit(solution)/shard_map/ppermute | solution.py:30
  75.5 4.2 collective-permute-start.4
  79.7 4.2 collective-permute-start.5
  83.9 4.2 collective-permute-start.6
  88.1 7.9 %collective-permute-start.7 = (f32[96,128]{1,0:T(8,128)S(1)}, f32[96,128]{1,0:T(8,128)S(1)}, u32[]{:S(2)}, u32[]{:S(2)}) collective-permute-start(f32[96,128]{1,0:T(8,128)S(1)} %add.223), channel_id=1, source_target_pairs={{0,16},{4,20},{8,24},{12,28},{16,0},{20,4},{24,8},{28,12},{1,17},{... | collective-permute-start | bytes 147464 | tf_op jit(solution)/shard_map/ppermute | solution.py:30
  96.6 54.2 %collective-permute-start.21 = (bf16[512,1024]{1,0:T(8,128)(2,1)}, bf16[512,1024]{1,0:T(8,128)(2,1)}, u32[]{:S(2)}, u32[]{:S(2)}) collective-permute-start(bf16[512,1024]{1,0:T(8,128)(2,1)} %param.12), channel_id=1, source_target_pairs={{0,2},{1,3},{2,0},{3,1},{4,6},{5,7},{6,4},{7,5},{8,10},{9,11},{10,... | collective-permute-start | bytes 3145736 | tf_op jit(solution)/shard_map/ppermute | solution.py:30
  99.1 38.9 %collective-permute-start.13 = (bf16[1024,256]{1,0:T(8,128)(2,1)}, bf16[1024,256]{1,0:T(8,128)(2,1)S(1)}, u32[]{:S(2)}, u32[]{:S(2)}) collective-permute-start(bf16[1024,256]{1,0:T(8,128)(2,1)} %collective-permute-done.12), channel_id=1, source_target_pairs={{0,1},{1,0},{2,3},{3,2},{4,5},{5,4},{6,7},{7,6},{8,9},{9,8},{10,11... | collective-permute-start | bytes 1572872 | tf_op jit(solution)/shard_map/ppermute | solution.py:30
  105.2 28.3 %copy-start = (bf16[2048,768]{1,0:T(8,128)(2,1)}, bf16[2048,768]{1,0:T(8,128)(2,1)S(1)}, u32[]{:S(2)}) copy-start(bf16[2048,768]{1,0:T(8,128)(2,1)S(1)} %add_convert_fusion.1.qkv_ref) | copy-start | bytes 9437188
  105.2 30.5 %copy-start.15 = (bf16[1024,1024]{1,0:T(8,128)(2,1)S(1)}, bf16[1024,1024]{1,0:T(8,128)(2,1)}, u32[]{:S(2)}) copy-start(bf16[1024,1024]{1,0:T(8,128)(2,1)} %constant_dynamic-update-slice_fusion.3) | copy-start | bytes 6291460
  133.6 15.7 %copy-start.10 = (bf16[512,256]{1,0:T(8,128)(2,1)}, bf16[512,256]{1,0:T(8,128)(2,1)S(1)}, u32[]{:S(2)}) copy-start(bf16[512,256]{1,0:T(8,128)(2,1)S(1)} %get-tuple-element.73) | copy-start | bytes 786436
  133.6 8.1 %collective-permute-start.10 = (bf16[512,256]{1,0:T(8,128)(2,1)S(1)}, bf16[512,256]{1,0:T(8,128)(2,1)S(1)}, u32[]{:S(2)}, u32[]{:S(2)}) collective-permute-start(bf16[512,256]{1,0:T(8,128)(2,1)S(1)} %get-tuple-element.74), channel_id=1, source_target_pairs={{0,3},{1,2},{2,1},{3,0},{4,7},{5,6},{6,5},{7,4},{8,11},{9,10},{10,... | collective-permute-start | bytes 786440 | tf_op jit(solution)/shard_map/ppermute | solution.py:30
  134.3 13.7 %collective-permute-start.9 = (bf16[512,256]{1,0:T(8,128)(2,1)S(1)}, bf16[512,256]{1,0:T(8,128)(2,1)S(1)}, u32[]{:S(2)}, u32[]{:S(2)}) collective-permute-start(bf16[512,256]{1,0:T(8,128)(2,1)S(1)} %get-tuple-element.75), channel_id=1, source_target_pairs={{0,2},{1,3},{2,0},{3,1},{4,6},{5,7},{6,4},{7,5},{8,10},{9,11},{10,... | collective-permute-start | bytes 786440 | tf_op jit(solution)/shard_map/ppermute | solution.py:30
  135.8 12.2 %collective-permute-start.8 = (bf16[512,256]{1,0:T(8,128)(2,1)S(1)}, bf16[512,256]{1,0:T(8,128)(2,1)S(1)}, u32[]{:S(2)}, u32[]{:S(2)}) collective-permute-start(bf16[512,256]{1,0:T(8,128)(2,1)S(1)} %get-tuple-element.76), channel_id=1, source_target_pairs={{0,1},{1,0},{2,3},{3,2},{4,5},{5,4},{6,7},{7,6},{8,9},{9,8},{10,11... | collective-permute-start | bytes 786440 | tf_op jit(solution)/shard_map/ppermute | solution.py:30
  138.1 11.3 %copy-start.16 = (bf16[1024,1024]{1,0:T(8,128)(2,1)}, bf16[1024,1024]{1,0:T(8,128)(2,1)S(1)}, u32[]{:S(2)}) copy-start(bf16[1024,1024]{1,0:T(8,128)(2,1)S(1)} %constant_dynamic-update-slice_fusion) | copy-start | bytes 6291460
  150.2 34.1 %copy-start.9 = (bf16[512,1024]{1,0:T(8,128)(2,1)}, bf16[512,1024]{1,0:T(8,128)(2,1)S(1)}, u32[]{:S(2)}) copy-start(bf16[512,1024]{1,0:T(8,128)(2,1)S(1)} %add_convert_fusion.5) | copy-start | bytes 3145732
  150.2 24.9 %collective-permute-start.15 = (bf16[512,1024]{1,0:T(8,128)(2,1)S(1)}, bf16[512,1024]{1,0:T(8,128)(2,1)}, u32[]{:S(2)}, u32[]{:S(2)}) collective-permute-start(bf16[512,1024]{1,0:T(8,128)(2,1)S(1)} %add_convert_fusion.5), channel_id=1, source_target_pairs={{0,2},{1,3},{2,0},{3,1},{4,6},{5,7},{6,4},{7,5},{8,10},{9,11},{10,... | collective-permute-start | bytes 3145736 | tf_op jit(solution)/shard_map/ppermute | solution.py:30
  150.8 26.7 %collective-permute-start.20 = (bf16[512,1024]{1,0:T(8,128)(2,1)}, bf16[512,1024]{1,0:T(8,128)(2,1)}, u32[]{:S(2)}, u32[]{:S(2)}) collective-permute-start(bf16[512,1024]{1,0:T(8,128)(2,1)} %param.12), channel_id=1, source_target_pairs={{0,1},{1,0},{2,3},{3,2},{4,5},{5,4},{6,7},{7,6},{8,9},{9,8},{10,11... | collective-permute-start | bytes 3145736 | tf_op jit(solution)/shard_map/ppermute | solution.py:30
  150.8 31.2 %collective-permute-start.22 = (bf16[512,1024]{1,0:T(8,128)(2,1)}, bf16[512,1024]{1,0:T(8,128)(2,1)}, u32[]{:S(2)}, u32[]{:S(2)}) collective-permute-start(bf16[512,1024]{1,0:T(8,128)(2,1)} %collective-permute-done.21), channel_id=1, source_target_pairs={{0,1},{1,0},{2,3},{3,2},{4,5},{5,4},{6,7},{7,6},{8,9},{9,8},{10,11... | collective-permute-start | bytes 3145736 | tf_op jit(solution)/shard_map/ppermute | solution.py:30
  151.3 33.0 %collective-permute-start.14 = (bf16[512,1024]{1,0:T(8,128)(2,1)S(1)}, bf16[512,1024]{1,0:T(8,128)(2,1)}, u32[]{:S(2)}, u32[]{:S(2)}) collective-permute-start(bf16[512,1024]{1,0:T(8,128)(2,1)S(1)} %add_convert_fusion.5), channel_id=1, source_target_pairs={{0,1},{1,0},{2,3},{3,2},{4,5},{5,4},{6,7},{7,6},{8,9},{9,8},{10,11... | collective-permute-start | bytes 3145736 | tf_op jit(solution)/shard_map/ppermute | solution.py:30
  175.1 9.2 %collective-permute-start.16 = (bf16[512,1024]{1,0:T(8,128)(2,1)}, bf16[512,1024]{1,0:T(8,128)(2,1)}, u32[]{:S(2)}, u32[]{:S(2)}) collective-permute-start(bf16[512,1024]{1,0:T(8,128)(2,1)} %collective-permute-done.15), channel_id=1, source_target_pairs={{0,1},{1,0},{2,3},{3,2},{4,5},{5,4},{6,7},{7,6},{8,9},{9,8},{10,11... | collective-permute-start | bytes 3145736 | tf_op jit(solution)/shard_map/ppermute | solution.py:30
  194.7 13.9 %copy-start.25 = (bf16[1024,1024]{1,0:T(8,128)(2,1)S(1)}, bf16[1024,1024]{1,0:T(8,128)(2,1)}, u32[]{:S(2)}) copy-start(bf16[1024,1024]{1,0:T(8,128)(2,1)} %all-gather.6.cloned.1.call-done) | copy-start | bytes 6291460
  214.4 9.8 %collective-permute-start.24 = (bf16[512,1024]{1,0:T(8,128)(2,1)}, bf16[512,1024]{1,0:T(8,128)(2,1)}, u32[]{:S(2)}, u32[]{:S(2)}) collective-permute-start(bf16[512,1024]{1,0:T(8,128)(2,1)} %get-tuple-element.61), channel_id=1, source_target_pairs={{0,1},{1,0},{2,3},{3,2},{4,5},{5,4},{6,7},{7,6},{8,9},{9,8},{10,11... | collective-permute-start | bytes 3145736 | tf_op jit(solution)/shard_map/ppermute | solution.py:30
  223.6 2.7 collective-permute-start.18
  223.7 4.6 collective-permute-start.23
  225.8 26.1 %collective-permute-start.25 = (bf16[512,1024]{1,0:T(8,128)(2,1)S(1)}, bf16[512,1024]{1,0:T(8,128)(2,1)S(1)}, u32[]{:S(2)}, u32[]{:S(2)}) collective-permute-start(bf16[512,1024]{1,0:T(8,128)(2,1)S(1)} %fusion.27), channel_id=1, source_target_pairs={{0,2},{1,3},{2,0},{3,1},{4,6},{5,7},{6,4},{7,5},{8,10},{9,11},{10,... | collective-permute-start | bytes 3145736 | tf_op jit(solution)/shard_map/ppermute | solution.py:30
  226.3 26.8 %collective-permute-start.17 = (bf16[512,1024]{1,0:T(8,128)(2,1)S(1)}, bf16[512,1024]{1,0:T(8,128)(2,1)S(1)}, u32[]{:S(2)}, u32[]{:S(2)}) collective-permute-start(bf16[512,1024]{1,0:T(8,128)(2,1)S(1)} %get-tuple-element.62), channel_id=1, source_target_pairs={{0,1},{1,0},{2,3},{3,2},{4,5},{5,4},{6,7},{7,6},{8,9},{9,8},{10,11... | collective-permute-start | bytes 3145736 | tf_op jit(solution)/shard_map/ppermute | solution.py:30
  226.7 46.8 %collective-permute-start.19 = (bf16[512,1024]{1,0:T(8,128)(2,1)S(1)}, bf16[512,1024]{1,0:T(8,128)(2,1)S(1)}, u32[]{:S(2)}, u32[]{:S(2)}) collective-permute-start(bf16[512,1024]{1,0:T(8,128)(2,1)S(1)} %fusion.29), channel_id=1, source_target_pairs={{0,2},{1,3},{2,0},{3,1},{4,6},{5,7},{6,4},{7,5},{8,10},{9,11},{10,... | collective-permute-start | bytes 3145736 | tf_op jit(solution)/shard_map/ppermute | solution.py:30
  276.9 14.6 %copy-start.4 = (f32[512,1024]{1,0:T(8,128)}, f32[512,1024]{1,0:T(8,128)S(1)}, u32[]{:S(2)}) copy-start(f32[512,1024]{1,0:T(8,128)S(1)} %get-tuple-element.55) | copy-start | bytes 6291460
  278.2 13.4 %copy-start.1 = (bf16[2048,768]{1,0:T(8,128)(2,1)S(1)}, bf16[2048,768]{1,0:T(8,128)(2,1)}, u32[]{:S(2)}) copy-start(bf16[2048,768]{1,0:T(8,128)(2,1)} %copy-done) | copy-start | bytes 9437188
  278.2 8.6 %collective-permute-start.28 = (bf16[512,256]{1,0:T(8,128)(2,1)S(1)}, bf16[512,256]{1,0:T(8,128)(2,1)S(1)}, u32[]{:S(2)}, u32[]{:S(2)}) collective-permute-start(bf16[512,256]{1,0:T(8,128)(2,1)S(1)} %get-tuple-element.70), channel_id=1, source_target_pairs={{0,3},{1,2},{2,1},{3,0},{4,7},{5,6},{6,5},{7,4},{8,11},{9,10},{10,... | collective-permute-start | bytes 786440 | tf_op jit(solution)/shard_map/ppermute | solution.py:30
  278.3 13.1 %collective-permute-start.27 = (bf16[512,256]{1,0:T(8,128)(2,1)S(1)}, bf16[512,256]{1,0:T(8,128)(2,1)S(1)}, u32[]{:S(2)}, u32[]{:S(2)}) collective-permute-start(bf16[512,256]{1,0:T(8,128)(2,1)S(1)} %get-tuple-element.71), channel_id=1, source_target_pairs={{0,2},{1,3},{2,0},{3,1},{4,6},{5,7},{6,4},{7,5},{8,10},{9,11},{10,... | collective-permute-start | bytes 786440 | tf_op jit(solution)/shard_map/ppermute | solution.py:30
  279.2 12.2 %collective-permute-start.26 = (bf16[512,256]{1,0:T(8,128)(2,1)S(1)}, bf16[512,256]{1,0:T(8,128)(2,1)S(1)}, u32[]{:S(2)}, u32[]{:S(2)}) collective-permute-start(bf16[512,256]{1,0:T(8,128)(2,1)S(1)} %get-tuple-element.72), channel_id=1, source_target_pairs={{0,1},{1,0},{2,3},{3,2},{4,5},{5,4},{6,7},{7,6},{8,9},{9,8},{10,11... | collective-permute-start | bytes 786440 | tf_op jit(solution)/shard_map/ppermute | solution.py:30
  332.8 15.3 %all-to-all-start.1 = ((f32[8,1,2560]{2,1,0:T(1,128)}), f32[8,1,2560]{2,1,0:T(1,128)S(1)}, u32[]{:S(2)}, u32[]{:S(2)}) async-start(f32[8,1,2560]{2,1,0:T(1,128)} %all_to_all.16), calls=%async_computation.1 | async-start | bytes 163840 | tf_op jit(solution)/shard_map/all_to_all | solution.py:548
  348.1 54.5 %all-to-all-start.2 = ((bf16[8,128,1024]{2,1,0:T(8,128)(2,1)}), bf16[8,128,1024]{2,1,0:T(8,128)(2,1)}, u32[]{:S(2)}, u32[]{:S(2)}) async-start(bf16[8,128,1024]{2,1,0:T(8,128)(2,1)} %bitcast.105), calls=%async_computation.2 | async-start | bytes 4194304 | tf_op jit(solution)/shard_map/all_to_all | solution.py:73
  365.4 41.6 %copy-start.11 = (bf16[512,256]{1,0:T(8,128)(2,1)S(1)}, bf16[512,256]{1,0:T(8,128)(2,1)}, u32[]{:S(2)}) copy-start(bf16[512,256]{1,0:T(8,128)(2,1)} %copy-done.10) | copy-start | bytes 786436
  402.6 52.2 %all-to-all-start.3 = ((bf16[8,128,1024]{2,1,0:T(8,128)(2,1)}), bf16[8,128,1024]{2,1,0:T(8,128)(2,1)}, u32[]{:S(2)}, u32[]{:S(2)}) async-start(bf16[8,128,1024]{2,1,0:T(8,128)(2,1)} %bitcast.104), calls=%async_computation.3 | async-start | bytes 4194304 | tf_op jit(solution)/shard_map/all_to_all | solution.py:73
  413.2 10.4 %collective-permute-start.32 = (bf16[1024,256]{0,1:T(8,128)(2,1)}, bf16[1024,256]{0,1:T(8,128)(2,1)}, u32[]{:S(2)}, u32[]{:S(2)}) collective-permute-start(bf16[1024,256]{0,1:T(8,128)(2,1)} %get-tuple-element.65), channel_id=1, source_target_pairs={{0,1},{1,0},{2,3},{3,2},{4,5},{5,4},{6,7},{7,6},{8,9},{9,8},{10,11... | collective-permute-start | bytes 1572872 | tf_op jit(solution)/shard_map/ppermute | solution.py:30
  413.2 7.3 %collective-permute-start.33 = (bf16[1024,256]{0,1:T(8,128)(2,1)}, bf16[1024,256]{0,1:T(8,128)(2,1)}, u32[]{:S(2)}, u32[]{:S(2)}) collective-permute-start(bf16[1024,256]{0,1:T(8,128)(2,1)} %get-tuple-element.66), channel_id=1, source_target_pairs={{0,1},{1,0},{2,3},{3,2},{4,5},{5,4},{6,7},{7,6},{8,9},{9,8},{10,11... | collective-permute-start | bytes 1572872 | tf_op jit(solution)/shard_map/ppermute | solution.py:30
  420.4 17.6 %copy-start.6 = (bf16[1024,768]{0,1:T(8,128)(2,1)S(1)}, bf16[1024,768]{0,1:T(8,128)(2,1)}, u32[]{:S(2)}) copy-start(bf16[1024,768]{0,1:T(8,128)(2,1)} %get-tuple-element.64) | copy-start | bytes 4718596
  420.4 43.7 %collective-permute-start.30 = (bf16[512,1024]{1,0:T(8,128)(2,1)}, bf16[512,1024]{1,0:T(8,128)(2,1)}, u32[]{:S(2)}, u32[]{:S(2)}) collective-permute-start(bf16[512,1024]{1,0:T(8,128)(2,1)} %get-tuple-element.59), channel_id=1, source_target_pairs={{0,1},{1,0},{2,3},{3,2},{4,5},{5,4},{6,7},{7,6},{8,9},{9,8},{10,11... | collective-permute-start | bytes 3145736 | tf_op jit(solution)/shard_map/ppermute | solution.py:30
  422.1 14.3 %collective-permute-start.34 = (bf16[1024,256]{0,1:T(8,128)(2,1)S(1)}, bf16[1024,256]{0,1:T(8,128)(2,1)S(1)}, u32[]{:S(2)}, u32[]{:S(2)}) collective-permute-start(bf16[1024,256]{0,1:T(8,128)(2,1)S(1)} %fusion.34), channel_id=1, source_target_pairs={{0,2},{1,3},{2,0},{3,1},{4,6},{5,7},{6,4},{7,5},{8,10},{9,11},{10,... | collective-permute-start | bytes 1572872 | tf_op jit(solution)/shard_map/ppermute | solution.py:30
  454.8 52.3 %all-to-all-start = ((bf16[8,128,1024]{1,2,0:T(8,128)(2,1)}), bf16[8,128,1024]{1,2,0:T(8,128)(2,1)S(1)}, u32[]{:S(2)}, u32[]{:S(2)}) async-start(bf16[8,128,1024]{1,2,0:T(8,128)(2,1)} %copy_bitcast_fusion), calls=%async_computation | async-start | bytes 4194304 | tf_op jit(solution)/shard_map/all_to_all | solution.py:73
  458.8 1.3 collective-permute-start.35
  460.1 3.9 collective-permute-start.36
  461.5 13.2 %collective-permute-start.29 = (bf16[512,1024]{1,0:T(8,128)(2,1)S(1)}, bf16[512,1024]{1,0:T(8,128)(2,1)}, u32[]{:S(2)}, u32[]{:S(2)}) collective-permute-start(bf16[512,1024]{1,0:T(8,128)(2,1)S(1)} %get-tuple-element.58), channel_id=1, source_target_pairs={{0,1},{1,0},{2,3},{3,2},{4,5},{5,4},{6,7},{7,6},{8,9},{9,8},{10,11... | collective-permute-start | bytes 3145736 | tf_op jit(solution)/shard_map/ppermute | solution.py:30
  466.3 24.5 %copy-start.3 = (bf16[512,1024]{1,0:T(8,128)(2,1)S(1)}, bf16[512,1024]{1,0:T(8,128)(2,1)}, u32[]{:S(2)}) copy-start(bf16[512,1024]{1,0:T(8,128)(2,1)} %param.11) | copy-start | bytes 3145732
  466.3 24.5 %copy-start.20 = (f32[512]{0:T(512)S(1)}, f32[512]{0:T(512)}, u32[]{:S(2)}) copy-start(f32[512]{0:T(512)} %copy-done.19) | copy-start | bytes 6148
  466.3 24.4 %copy-start.23 = (f32[512]{0:T(512)S(1)}, f32[512]{0:T(512)}, u32[]{:S(2)}) copy-start(f32[512]{0:T(512)} %copy-done.22) | copy-start | bytes 6148
  466.3 24.4 %collective-permute-start.31 = (bf16[512,1024]{1,0:T(8,128)(2,1)S(1)}, bf16[512,1024]{1,0:T(8,128)(2,1)S(1)}, u32[]{:S(2)}, u32[]{:S(2)}) collective-permute-start(bf16[512,1024]{1,0:T(8,128)(2,1)S(1)} %fusion.24), channel_id=1, source_target_pairs={{0,2},{1,3},{2,0},{3,1},{4,6},{5,7},{6,4},{7,5},{8,10},{9,11},{10,... | collective-permute-start | bytes 3145736 | tf_op jit(solution)/shard_map/ppermute | solution.py:30
  474.7 19.0 %copy-start.5 = (f32[512,1024]{1,0:T(8,128)S(1)}, f32[512,1024]{1,0:T(8,128)}, u32[]{:S(2)}) copy-start(f32[512,1024]{1,0:T(8,128)} %copy-done.4) | copy-start | bytes 6291460
  (11 other events, 31.9 us)
Sparse Core Ops, SparseCore 0:
  10.7 50.6 all-gather.3
  63.5 47.1 all-gather.5
  112.8 48.0 all-gather.7
